TPU v7x, 32 devices: a whole 2x2x4 slice. The times are simulated.
32 devices in a mesh: gx: 4 (over x, core), gy: 2 (over y), gz: 4 (over z).
Axes of the slice: x: 2, y: 2, z: 4, core: 2. Of those that a mesh axis runs over, the one named last changes fastest.
Arguments:
- hamiltonian: float32 [4, 2, 4, 7, 384, 384], P('gx', 'gy', 'gz'), may hold values from -20 to 20, as said below
- keep_mask: int32 [4, 2, 4, 7], P('gx', 'gy', 'gz'), may hold values from 0 to 1, as said below
Outputs:
- sign_blocks: float32 [4, 2, 4, 7, 384, 384], P('gx', 'gy', 'gz')
Inputs may be any that keep to these rules, and one draw needn't show every extreme that they name: `hamiltonian`: entries are real numbers; the blocks are dense. `keep_mask`: slot 0 is 1 for every domain.
All inputs are finite; a program needn't handle non-finite values.
Results may differ from a plain program's by a relative error of at most 0.00025.
Values sent between devices are 32-bit elements; how exact they have to be, the bound alone decides.
No kernel may reach another device: no remote copies, remote signals or barrier semaphores. Data moves between devices by JAX's collectives and lax.ppermute only.
A program may use at most 128 MiB of HBM per device.

v0:
```python
import jax
import jax.numpy as jnp
from jax import lax
from jax.experimental import pallas as pl
from jax.experimental.pallas import tpu as pltpu
from jax.sharding import PartitionSpec as P

TARGET_RMS = 1.0
SIDES = (("gz", 5), ("gy", 3), ("gx", 1))
LOCAL_ORDER = (("gx", 1), ("gy", 3), ("gz", 5))
SCALE = 2.0**30
KEEP_ROWS = 8
WORD = jnp.float32
HALF = jnp.bfloat16
VMEM_BYTES = 16 * 2**20


def passed_along(value, axis, steps):
    count = lax.axis_size(axis)
    pairs = [(source, (source + steps) % count) for source in range(count)]
    return lax.ppermute(value, axis, pairs)


def partners_along(picked, axis):
    if lax.axis_size(axis) == 2:
        both = passed_along(picked[0], axis, 1)
        return (both, 1), (both, 0)
    return (
        (passed_along(picked[1], axis, -1), None),
        (passed_along(picked[0], axis, 1), None),
    )


def faces_along(block, axis):
    if lax.axis_size(axis) == 2:
        face = passed_along(block, axis, 1)
        return face, face
    return (passed_along(block, axis, -1), passed_along(block, axis, 1))


def summed_over(value, axis):
    total = value
    for step in range(1, lax.axis_size(axis)):
        total = total + passed_along(value, axis, step)
    return total


HBM = pl.BlockSpec(memory_space=pltpu.HBM)
VMEM = pl.BlockSpec(memory_space=pltpu.VMEM)
SMEM = pl.BlockSpec(memory_space=pltpu.SMEM)
PARAMS = pltpu.CompilerParams(vmem_limit_bytes=VMEM_BYTES)


def struct(*shape, dtype=WORD):
    return jax.ShapeDtypeStruct(shape, dtype)


def split(value):
    high = value.astype(HALF)
    return high, (value - high.astype(WORD)).astype(HALF)


def dot3(left, right):
    def dot(a, b):
        return jnp.dot(a, b, preferred_element_type=WORD)

    return dot(left[0], right[0]) + (dot(left[0], right[1]) + dot(left[1], right[0]))


def both(pair, s):
    return pair[0][s], pair[1][s]


def pick_pair(raw, slot, joined):
    width = raw.shape[-1]
    block = struct(width, width)
    shapes = [struct(2, width, width)] if joined else [block, block]

    def kernel(raw_ref, *rest):
        sem = rest[-1]
        copies = []
        for index, out in enumerate(rest[:-1]):
            source = raw_ref.at[pl.ds(slot, 2)] if joined else raw_ref.at[slot + index]
            copies.append(pltpu.make_async_copy(source, out, sem.at[index]))
        for copy in copies:
            copy.start()
        for copy in copies:
            copy.wait()

    return pl.pallas_call(
        kernel,
        in_specs=[HBM],
        out_specs=[VMEM] * len(shapes),
        out_shape=shapes,
        scratch_shapes=[pltpu.SemaphoreType.DMA((len(shapes),))],
        compiler_params=PARAMS,
    )(raw)


def pick_own(raw, keep):
    slots, width = raw.shape[0], raw.shape[-1]

    def kernel(raw_ref, keep_ref, out, sem):
        copy = pltpu.make_async_copy(raw_ref.at[0], out.at[pl.ds(0, width)], sem.at[0])
        copy.start()
        row = lax.broadcasted_iota(jnp.int32, (KEEP_ROWS, width), 0)
        tile = jnp.zeros((KEEP_ROWS, width), WORD)
        for s in range(slots):
            tile = jnp.where(row == s, keep_ref[s].astype(WORD), tile)
        out[pl.ds(width, KEEP_ROWS), :] = tile
        copy.wait()

    return pl.pallas_call(
        kernel,
        in_specs=[HBM, SMEM],
        out_specs=VMEM,
        out_shape=struct(width + KEEP_ROWS, width),
        scratch_shapes=[pltpu.SemaphoreType.DMA((1,))],
        compiler_params=PARAMS,
        name="pick_own",
    )(raw, keep)


def first_kernel(block_ref, high_ref, low_ref, product_ref, sum_ref, total):
    s = pl.program_id(0)
    raw = block_ref[0]
    half = split(raw * SCALE)
    high_ref[s], low_ref[s] = half

    @pl.when(s == 0)
    def _():
        total[...] = jnp.zeros_like(total)

    product_ref[s] = dot3((high_ref[0], low_ref[0]), half)
    rows = total.shape[0]
    total[...] += jnp.sum((raw * raw).reshape(-1, rows, raw.shape[-1]), axis=0)

    @pl.when(s == pl.num_programs(0) - 1)
    def _():
        sum_ref[0] = jnp.sum(total[...])


def first_products(raw):
    slots, width = raw.shape[0], raw.shape[-1]
    return pl.pallas_call(
        first_kernel,
        grid=(slots,),
        in_specs=[pl.BlockSpec((1, width, width), lambda s: (s, 0, 0))],
        out_specs=[VMEM, VMEM, VMEM, SMEM],
        out_shape=[
            struct(*raw.shape, dtype=HALF),
            struct(*raw.shape, dtype=HALF),
            struct(*raw.shape),
            struct(1),
        ],
        scratch_shapes=[pltpu.VMEM((8, width), WORD)],
        compiler_params=PARAMS,
        name="first_products",
    )(raw)


def side_products(halves, slot, partners, products=None, others=()):
    width = halves[0].shape[-1]
    operands = [*halves, partners[0][0], partners[1][0]]
    out_shape = [struct(2, width, width)]
    if products is not None:
        operands += [products, *others]
        out_shape.append(struct(width, width))

    def kernel(high, low, first, second, *rest):
        values = []
        for index, (ref, (_, part)) in enumerate(zip((first, second), partners)):
            value = ref[...] if part is None else ref[part]
            values.append(dot3(both((high, low), slot + index), split(value * SCALE)))
        if products is None:
            (side_ref,) = rest
        else:
            own, *sides, side_ref, square_ref = rest
            total = own[0]
            for other in sides:
                total = total + (other[0] + other[1])
            square_ref[...] = total + (values[0] + values[1])
        side_ref[0] = values[0]
        side_ref[1] = values[1]

    return pl.pallas_call(
        kernel,
        in_specs=[VMEM] * len(operands),
        out_specs=[VMEM] * len(out_shape),
        out_shape=out_shape,
        compiler_params=PARAMS,
    )(*operands)


def cube_parts(keep, halves, slot, faces, partners, products, side):
    width = halves[0].shape[-1]

    def kernel(keep_ref, high, low, f0, f1, p0, p1, products, side, pair, near, mix):
        nears, mixes = [], []
        for index, (face, ref, (_, part)) in enumerate(
            zip((f0, f1), (p0, p1), partners)
        ):
            s = slot + index
            back = width + slot + 1 - index
            kept = face[back : back + 1, :]
            value = ref[...] if part is None else ref[part]
            coupled = dot3(both((high, low), s), split(face[:width] * SCALE))
            square = keep_ref[s].astype(WORD) * (products[s] + coupled)
            pair[index] = dot3(both((high, low), 0), split(square))
            nears.append(dot3(split(kept * coupled), split(value * SCALE)))
            mixes.append(kept * side[index])
        near[...] = nears[0] + nears[1]
        mix[...] = mixes[0] + mixes[1]

    return pl.pallas_call(
        kernel,
        in_specs=[SMEM] + [VMEM] * 8,
        out_specs=[VMEM] * 3,
        out_shape=[
            struct(2, width, width),
            struct(width, width),
            struct(width, width),
        ],
        compiler_params=PARAMS,
    )(keep, *halves, *faces, partners[0][0], partners[1][0], products, side)


def own_cube(halves, square, parts):
    width = square.shape[-1]

    def kernel(high, low, square_ref, *rest):
        *refs, out = rest
        near, mix = refs[0][...], refs[1][...]
        for ref in refs[2::2]:
            near = near + ref[...]
        for ref in refs[3::2]:
            mix = mix + ref[...]
        own = both((high, low), 0)
        out[...] = dot3(own, split(square_ref[...])) + (dot3(split(mix), own) + near)

    return pl.pallas_call(
        kernel,
        in_specs=[VMEM] * (3 + len(parts)),
        out_specs=VMEM,
        out_shape=struct(width, width),
        compiler_params=PARAMS,
        name="own_cube",
    )(*halves, square, *parts)


def weighted(scalars, keep, raw, cube):
    small = scalars[1]
    kept = keep.astype(WORD)
    return kept * ((1.5 * scalars[0]) * raw - 0.5 * (((cube * small) * small) * small))


def own_output(scalars, keep, raw, cube):
    width = raw.shape[-1]
    block = pl.BlockSpec((1, width, width), lambda i: (0, 0, 0))

    def kernel(scalars, keep_ref, raw_ref, cube_ref, out):
        out[0] = weighted(scalars, keep_ref[0], raw_ref[0], cube_ref[...])

    return pl.pallas_call(
        kernel,
        grid=(1,),
        in_specs=[SMEM, SMEM, block, VMEM],
        out_specs=block,
        out_shape=struct(*raw.shape),
        compiler_params=PARAMS,
        name="own_output",
    )(scalars, keep, raw, cube)


def pair_output(scalars, keep, halves, raw, slot, square_faces, part, out):
    width = raw.shape[-1]
    block = pl.BlockSpec((1, width, width), lambda i: (slot + i, 0, 0))

    def kernel(scalars, keep_ref, high, low, raw_ref, f0, f1, part_ref, _, out_ref):
        for index, face in enumerate((f0, f1)):

            @pl.when(pl.program_id(0) == index)
            def _(index=index, face=face):
                s = slot + index
                cube = part_ref[index] + dot3(both((high, low), s), split(face[...]))
                out_ref[0] = weighted(scalars, keep_ref[s], raw_ref[0], cube)

    return pl.pallas_call(
        kernel,
        grid=(2,),
        in_specs=[SMEM, SMEM, VMEM, VMEM, block, VMEM, VMEM, VMEM, HBM],
        out_specs=block,
        out_shape=struct(*raw.shape),
        input_output_aliases={8: 0},
        compiler_params=PARAMS,
    )(scalars, keep, *halves, raw, *square_faces, part, out)


def body(hamiltonian, keep_mask):
    return step(hamiltonian[0, 0, 0], keep_mask[0, 0, 0])[None, None, None]


def step(raw, keep):
    entry_count = raw.shape[-1]
    for axis, _ in SIDES:
        entry_count = entry_count * lax.axis_size(axis)

    partners, faces, square_faces, side, parts = {}, {}, {}, {}, {}
    for axis, slot in SIDES:
        picked = pick_pair(raw, slot, lax.axis_size(axis) == 2)
        partners[slot] = partners_along(picked, axis)
    own = pick_own(raw, keep)
    for axis, slot in SIDES:
        faces[slot] = faces_along(own, axis)

    high, low, products, squares = first_products(raw)
    halves = (high, low)
    norm_sq = squares[0]
    for axis, _ in SIDES:
        norm_sq = summed_over(norm_sq, axis)
    factor = TARGET_RMS / jnp.sqrt(norm_sq / entry_count)
    scalars = jnp.stack([factor, factor * (1.0 / SCALE)])

    for axis, slot in LOCAL_ORDER[:-1]:
        (side[slot],) = side_products(halves, slot, partners[slot])
    slot = LOCAL_ORDER[-1][1]
    side[slot], square = side_products(
        halves, slot, partners[slot], products, tuple(side.values())
    )
    for axis, slot in SIDES:
        square_faces[slot] = faces_along(square, axis)

    sums = []
    for axis, slot in LOCAL_ORDER:
        parts[slot], near, mix = cube_parts(
            keep, halves, slot, faces[slot], partners[slot], products, side[slot]
        )
        sums += [near, mix]
    cube = own_cube(halves, square, sums)
    out = own_output(scalars, keep, raw, cube)
    for axis, slot in LOCAL_ORDER:
        out = pair_output(
            scalars, keep, halves, raw, slot, square_faces[slot], parts[slot], out
        )
    return out


def solution(mesh):
    placed = (P("gx", "gy", "gz", None, None, None), P("gx", "gy", "gz", None))
    return jax.shard_map(
        body,
        mesh=mesh,
        in_specs=placed,
        out_specs=P("gx", "gy", "gz", None, None, None),
        check_vma=False,
    )
```

profile of v0, /device:TPU:0, one launch (start us, length us, event | category | flops | bytes accessed | tf_op | source)
XLA Modules:
  0.0 130.9 jit_solution(6605928804781686993)
XLA Ops:
  0.0 2.2 %copy-done = f32[1,1,1,7,384,384]{5,4,3,2,1,0:T(8,128)S(1)} copy-done((f32[1,1,1,7,384,384]{5,4,3,2,1,0:T(8,128)S(1)}, f32[1,1,1,7,384,384]{5,4,3,2,1,0:T(8,128)}, u32[]{:S(2)}) %copy-start) | copy-done | bytes 4128792
  3.4 3.1 %collective-permute-start.11 = (f32[2,384,384]{2,1,0:T(8,128)}, f32[2,384,384]{2,1,0:T(8,128)S(1)}, u32[]{:S(2)}, u32[]{:S(2)}) collective-permute-start(f32[2,384,384]{2,1,0:T(8,128)} %shard_map.31), channel_id=1, source_target_pairs={{0,4},{4,0},{1,5},{5,1},{2,6},{6,2},{3,7},{7,3},{8,12},{12,8},{9,1... | collective-permute-start | bytes 3538952 | tf_op jit(solution)/shard_map/ppermute | solution.py:21
  6.5 6.9 %first_products.1 = (bf16[7,384,384]{2,1,0:T(8,128)(2,1)S(1)}, bf16[7,384,384]{2,1,0:T(8,128)(2,1)S(1)}, f32[7,384,384]{2,1,0:T(8,128)S(1)}, f32[1]{0:T(128)}) custom-call(f32[7,384,384]{2,1,0:T(8,128)S(1)} %bitcast.7), custom_call_target="tpu_custom_call" | custom-call | tf_op jit(solution)/shard_map/first_products/pallas_call | solution.py:145
  16.3 2.6 %collective-permute-start.1 = (f32[]{:T(128)}, f32[]{:T(128)}, u32[]{:S(2)}, u32[]{:S(2)}) collective-permute-start(f32[]{:T(128)} %bitcast.1), channel_id=1, source_target_pairs={{0,2},{1,3},{2,0},{3,1},{4,6},{5,7},{6,4},{7,5},{8,10},{9,11},{10,... | collective-permute-start | bytes 20 | tf_op jit(solution)/shard_map/ppermute | solution.py:21
  23.6 1.7 %collective-permute-start.9 = (f32[384,384]{1,0:T(8,128)}, f32[384,384]{1,0:T(8,128)}, u32[]{:S(2)}, u32[]{:S(2)}) collective-permute-start(f32[384,384]{1,0:T(8,128)} %get-tuple-element.30), channel_id=1, source_target_pairs={{0,24},{8,0},{16,8},{24,16},{1,25},{9,1},{17,9},{25,17},{2,26},{10... | collective-permute-start | bytes 1769480 | tf_op jit(solution)/shard_map/ppermute | solution.py:21
  28.4 3.7 %collective-permute-start.3 = (f32[]{:T(128)}, f32[]{:T(128)}, u32[]{:S(2)}, u32[]{:S(2)}) collective-permute-start(f32[]{:T(128)} %add.23), channel_id=1, source_target_pairs={{0,4},{4,0},{1,5},{5,1},{2,6},{6,2},{3,7},{7,3},{8,12},{12,8},{9,1... | collective-permute-start | bytes 20 | tf_op jit(solution)/shard_map/ppermute | solution.py:21
  34.2 2.1 %collective-permute-done.4 = f32[]{:T(128)} collective-permute-done((f32[]{:T(128)}, f32[]{:T(128)}, u32[]{:S(2)}, u32[]{:S(2)}) %collective-permute-start.4) | collective-permute-done | bytes 36 | tf_op jit(solution)/shard_map/ppermute | solution.py:21
  36.4 3.0 %collective-permute-start.5 = (f32[]{:T(128)}, f32[]{:T(128)}, u32[]{:S(2)}, u32[]{:S(2)}) collective-permute-start(f32[]{:T(128)} %add.24), channel_id=1, source_target_pairs={{0,16},{8,24},{16,0},{24,8},{1,17},{9,25},{17,1},{25,9},{2,18},{10... | collective-permute-start | bytes 20 | tf_op jit(solution)/shard_map/ppermute | solution.py:21
  41.2 1.8 %collective-permute-start.8 = (f32[384,384]{1,0:T(8,128)}, f32[384,384]{1,0:T(8,128)S(1)}, u32[]{:S(2)}, u32[]{:S(2)}) collective-permute-start(f32[384,384]{1,0:T(8,128)} %copy-done.28), channel_id=1, source_target_pairs={{0,1},{1,2},{2,3},{3,0},{4,5},{5,6},{6,7},{7,4},{8,9},{9,10},{10,1... | collective-permute-start | bytes 1769480 | tf_op jit(solution)/shard_map/ppermute | solution.py:21
  43.0 2.2 %copy-done.1 = f32[1,1,1,7,384,384]{5,4,3,2,1,0:T(8,128)S(1)} copy-done((f32[1,1,1,7,384,384]{5,4,3,2,1,0:T(8,128)S(1)}, f32[1,1,1,7,384,384]{5,4,3,2,1,0:T(8,128)}, u32[]{:S(2)}) %copy-start.1) | copy-done | bytes 4128792
  48.9 9.7 %collective-permute-done.8.second.p1 = f32[384,384]{1,0:T(8,128)S(1)} collective-permute-done((f32[384,384]{1,0:T(8,128)}, f32[384,384]{1,0:T(8,128)S(1)}, u32[]{:S(2)}, u32[]{:S(2)}) %collective-permute-start.8) | collective-permute-done | bytes 589856 | tf_op jit(solution)/shard_map/ppermute | solution.py:21
  58.6 2.3 %collective-permute-start.14 = (f32[392,384]{1,0:T(8,128)S(1)}, f32[392,384]{1,0:T(8,128)S(1)}, u32[]{:S(2)}, u32[]{:S(2)}) collective-permute-start(f32[392,384]{1,0:T(8,128)S(1)} %pick_own.1), channel_id=1, source_target_pairs={{0,3},{1,0},{2,1},{3,2},{4,7},{5,4},{6,5},{7,6},{8,11},{9,8},{10,9... | collective-permute-start | bytes 1806344 | tf_op jit(solution)/shard_map/ppermute | solution.py:21
  60.9 2.5 %shard_map.30.rest_1_.side = f32[2,384,384]{2,1,0:T(8,128)S(1)} custom-call(bf16[7,384,384]{2,1,0:T(8,128)(2,1)S(1)} %get-tuple-element.25.high, bf16[7,384,384]{2,1,0:T(8,128)(2,1)S(1)} %copy-done.4, f32[384,384]{1,0:T(8,128)} %collective-permute-done.9.first.p0, f32[384,384]{1,0:T(8,128)} %collective-permute-done.10.second.p1), custom_call_target="tpu_custom_call" | custom-call | tf_op jit(solution)/shard_map/pallas_call | solution.py:186
  66.4 3.2 %shard_map.33 = (f32[2,384,384]{2,1,0:T(8,128)S(1)}, f32[384,384]{1,0:T(8,128)}) custom-call(bf16[7,384,384]{2,1,0:T(8,128)(2,1)S(1)} %get-tuple-element.25.high, bf16[7,384,384]{2,1,0:T(8,128)(2,1)S(1)} %copy-done.4, f32[384,384]{1,0:T(8,128)} %collective-permute-done.7.first.p0, f32[384,384]{1,0:T(8,128)S(1)} %collective-permute-done.8.second.p1, ...), custom_call_target="tpu_custom_call" | custom-call | tf_op jit(solution)/shard_map/pallas_call | solution.py:186
  76.3 3.7 %collective-permute-start.12 = (f32[384,384]{1,0:T(8,128)}, f32[384,384]{1,0:T(8,128)}, u32[]{:S(2)}, u32[]{:S(2)}) collective-permute-start(f32[384,384]{1,0:T(8,128)} %get-tuple-element.32.square_ref), channel_id=1, source_target_pairs={{0,3},{1,0},{2,1},{3,2},{4,7},{5,4},{6,5},{7,6},{8,11},{9,8},{10,9... | collective-permute-start | bytes 1769480 | tf_op jit(solution)/shard_map/ppermute | solution.py:21
  80.0 8.7 %collective-permute-done.15.f1 = f32[392,384]{1,0:T(8,128)S(1)} collective-permute-done((f32[392,384]{1,0:T(8,128)S(1)}, f32[392,384]{1,0:T(8,128)S(1)}, u32[]{:S(2)}, u32[]{:S(2)}) %collective-permute-start.15) | collective-permute-done | bytes 602144 | tf_op jit(solution)/shard_map/ppermute | solution.py:21
  94.8 2.2 %copy-done.8 = f32[7,384,384]{2,1,0:T(8,128)S(1)} copy-done((f32[7,384,384]{2,1,0:T(8,128)S(1)}, f32[7,384,384]{2,1,0:T(8,128)}, u32[]{:S(2)}) %copy-start.8) | copy-done | bytes 4128792
  100.3 5.3 %shard_map.36 = (f32[2,384,384]{2,1,0:T(8,128)S(1)}, f32[384,384]{1,0:T(8,128)S(1)}, f32[384,384]{1,0:T(8,128)S(1)}) custom-call(s32[7]{0:T(128)S(1)} %bitcast.16, bf16[7,384,384]{2,1,0:T(8,128)(2,1)S(1)} %get-tuple-element.25.high, bf16[7,384,384]{2,1,0:T(8,128)(2,1)S(1)} %copy-done.5, f32[392,384]{1,0:T(8,128)S(1)} %copy-done.20, ...), custom_call_target="tpu_custom_call" | custom-call | tf_op jit(solution)/shard_map/pallas_call | solution.py:215
  105.7 4.5 %shard_map.35 = (f32[2,384,384]{2,1,0:T(8,128)S(1)}, f32[384,384]{1,0:T(8,128)S(1)}, f32[384,384]{1,0:T(8,128)S(1)}) custom-call(s32[7]{0:T(128)S(1)} %bitcast.17, bf16[7,384,384]{2,1,0:T(8,128)(2,1)S(1)} %get-tuple-element.25.high, bf16[7,384,384]{2,1,0:T(8,128)(2,1)S(1)} %copy-done.5, f32[392,384]{1,0:T(8,128)S(1)} %copy-done.14, ...), custom_call_target="tpu_custom_call" | custom-call | tf_op jit(solution)/shard_map/pallas_call | solution.py:215
  110.3 5.0 %shard_map.34 = (f32[2,384,384]{2,1,0:T(8,128)S(1)}, f32[384,384]{1,0:T(8,128)S(1)}, f32[384,384]{1,0:T(8,128)S(1)}) custom-call(s32[7]{0:T(128)S(1)} %bitcast.18, bf16[7,384,384]{2,1,0:T(8,128)(2,1)S(1)} %get-tuple-element.25.high, bf16[7,384,384]{2,1,0:T(8,128)(2,1)S(1)} %copy-done.5, f32[392,384]{1,0:T(8,128)S(1)} %copy-done.22, ...), custom_call_target="tpu_custom_call" | custom-call | tf_op jit(solution)/shard_map/pallas_call | solution.py:215
  115.3 2.5 %own_cube.1.cube_ref = f32[384,384]{1,0:T(8,128)S(1)} custom-call(bf16[7,384,384]{2,1,0:T(8,128)(2,1)S(1)} %get-tuple-element.25.high, bf16[7,384,384]{2,1,0:T(8,128)(2,1)S(1)} %copy-done.5, f32[384,384]{1,0:T(8,128)} %get-tuple-element.32.square_ref, f32[384,384]{1,0:T(8,128)S(1)} %get-tuple-element.37.rest_0_, f32[384,384]{1,0:T(8,128)S(1)} %get-tuple-element.38.rest_1_, ...), custom_call_target="tpu_custom_call" | custom-call | tf_op jit(solution)/shard_map/own_cube/pallas_call | solution.py:241
  119.4 4.0 %shard_map.37._ = f32[7,384,384]{2,1,0:T(8,128)} custom-call(f32[2]{0:T(128)S(1)} %pad_maximum_fusion.scalars, s32[7]{0:T(128)S(1)} %bitcast.20, bf16[7,384,384]{2,1,0:T(8,128)(2,1)S(1)} %get-tuple-element.25.high, bf16[7,384,384]{2,1,0:T(8,128)(2,1)S(1)} %copy-done.5, f32[7,384,384]{2,1,0:T(8,128)S(1)} %bitcast.12, ...), custom_call_target="tpu_custom_call", output_to_operand_aliasing={{}: (8, {})} | custom-call | tf_op jit(solution)/shard_map/pallas_call | solution.py:288
  123.4 3.7 %shard_map.38._ = f32[7,384,384]{2,1,0:T(8,128)} custom-call(f32[2]{0:T(128)S(1)} %pad_maximum_fusion.scalars, s32[7]{0:T(128)S(1)} %bitcast.21, bf16[7,384,384]{2,1,0:T(8,128)(2,1)S(1)} %get-tuple-element.25.high, bf16[7,384,384]{2,1,0:T(8,128)(2,1)S(1)} %copy-done.5, f32[7,384,384]{2,1,0:T(8,128)S(1)} %bitcast.13, ...), custom_call_target="tpu_custom_call", output_to_operand_aliasing={{}: (8, {})} | custom-call | tf_op jit(solution)/shard_map/pallas_call | solution.py:288
  127.1 3.8 %shard_map.39 = f32[7,384,384]{2,1,0:T(8,128)} custom-call(f32[2]{0:T(128)S(1)} %pad_maximum_fusion.scalars, s32[7]{0:T(128)S(1)} %bitcast.22, bf16[7,384,384]{2,1,0:T(8,128)(2,1)S(1)} %get-tuple-element.25.high, bf16[7,384,384]{2,1,0:T(8,128)(2,1)S(1)} %copy-done.5, f32[7,384,384]{2,1,0:T(8,128)S(1)} %bitcast.14, ...), custom_call_target="tpu_custom_call", output_to_operand_aliasing={{}: (8, {})} | custom-call | tf_op jit(solution)/shard_map/pallas_call | solution.py:288
  (97 shorter events, 35.1 us)
Async XLA Ops:
  3.4 57.4 %collective-permute-start.11 = (f32[2,384,384]{2,1,0:T(8,128)}, f32[2,384,384]{2,1,0:T(8,128)S(1)}, u32[]{:S(2)}, u32[]{:S(2)}) collective-permute-start(f32[2,384,384]{2,1,0:T(8,128)} %shard_map.31), channel_id=1, source_target_pairs={{0,4},{4,0},{1,5},{5,1},{2,6},{6,2},{3,7},{7,3},{8,12},{12,8},{9,1... | collective-permute-start | bytes 3538952 | tf_op jit(solution)/shard_map/ppermute | solution.py:21
  14.8 8.9 %collective-permute-start = (f32[]{:T(128)}, f32[]{:T(128)}, u32[]{:S(2)}, u32[]{:S(2)}) collective-permute-start(f32[]{:T(128)} %bitcast.1), channel_id=1, source_target_pairs={{0,1},{1,2},{2,3},{3,0},{4,5},{5,6},{6,7},{7,4},{8,9},{9,10},{10,1... | collective-permute-start | bytes 20 | tf_op jit(solution)/shard_map/ppermute | solution.py:21
  16.3 10.3 %collective-permute-start.1 = (f32[]{:T(128)}, f32[]{:T(128)}, u32[]{:S(2)}, u32[]{:S(2)}) collective-permute-start(f32[]{:T(128)} %bitcast.1), channel_id=1, source_target_pairs={{0,2},{1,3},{2,0},{3,1},{4,6},{5,7},{6,4},{7,5},{8,10},{9,11},{10,... | collective-permute-start | bytes 20 | tf_op jit(solution)/shard_map/ppermute | solution.py:21
  18.9 8.8 %collective-permute-start.2 = (f32[]{:T(128)}, f32[]{:T(128)}, u32[]{:S(2)}, u32[]{:S(2)}) collective-permute-start(f32[]{:T(128)} %bitcast.1), channel_id=1, source_target_pairs={{0,3},{1,0},{2,1},{3,2},{4,7},{5,4},{6,5},{7,6},{8,11},{9,8},{10,9... | collective-permute-start | bytes 20 | tf_op jit(solution)/shard_map/ppermute | solution.py:21
  21.6 21.4 %copy-start.27 = (s32[1,1,1,7]{3,2,1,0:T(1,128)S(1)}, s32[1,1,1,7]{3,2,1,0:T(1,128)}, u32[]{:S(2)}) copy-start(s32[1,1,1,7]{3,2,1,0:T(1,128)} %param.3) | copy-start | bytes 88
  21.6 24.2 %collective-permute-start.10 = (f32[384,384]{1,0:T(8,128)}, f32[384,384]{1,0:T(8,128)}, u32[]{:S(2)}, u32[]{:S(2)}) collective-permute-start(f32[384,384]{1,0:T(8,128)} %get-tuple-element.31), channel_id=1, source_target_pairs={{0,8},{8,16},{16,24},{24,0},{1,9},{9,17},{17,25},{25,1},{2,10},{10... | collective-permute-start | bytes 1769480 | tf_op jit(solution)/shard_map/ppermute | solution.py:21
  23.6 23.6 %collective-permute-start.9 = (f32[384,384]{1,0:T(8,128)}, f32[384,384]{1,0:T(8,128)}, u32[]{:S(2)}, u32[]{:S(2)}) collective-permute-start(f32[384,384]{1,0:T(8,128)} %get-tuple-element.30), channel_id=1, source_target_pairs={{0,24},{8,0},{16,8},{24,16},{1,25},{9,1},{17,9},{25,17},{2,26},{10... | collective-permute-start | bytes 1769480 | tf_op jit(solution)/shard_map/ppermute | solution.py:21
  26.6 20.7 %collective-permute-start.7 = (f32[384,384]{1,0:T(8,128)}, f32[384,384]{1,0:T(8,128)}, u32[]{:S(2)}, u32[]{:S(2)}) collective-permute-start(f32[384,384]{1,0:T(8,128)} %copy-done.29), channel_id=1, source_target_pairs={{0,3},{1,0},{2,1},{3,2},{4,7},{5,4},{6,5},{7,6},{8,11},{9,8},{10,9... | collective-permute-start | bytes 1769480 | tf_op jit(solution)/shard_map/ppermute | solution.py:21
  28.4 4.4 %collective-permute-start.3 = (f32[]{:T(128)}, f32[]{:T(128)}, u32[]{:S(2)}, u32[]{:S(2)}) collective-permute-start(f32[]{:T(128)} %add.23), channel_id=1, source_target_pairs={{0,4},{4,0},{1,5},{5,1},{2,6},{6,2},{3,7},{7,3},{8,12},{12,8},{9,1... | collective-permute-start | bytes 20 | tf_op jit(solution)/shard_map/ppermute | solution.py:21
  33.4 3.0 %collective-permute-start.4 = (f32[]{:T(128)}, f32[]{:T(128)}, u32[]{:S(2)}, u32[]{:S(2)}) collective-permute-start(f32[]{:T(128)} %add.24), channel_id=1, source_target_pairs={{0,8},{8,16},{16,24},{24,0},{1,9},{9,17},{17,25},{25,1},{2,10},{10... | collective-permute-start | bytes 20 | tf_op jit(solution)/shard_map/ppermute | solution.py:21
  36.4 3.5 %collective-permute-start.5 = (f32[]{:T(128)}, f32[]{:T(128)}, u32[]{:S(2)}, u32[]{:S(2)}) collective-permute-start(f32[]{:T(128)} %add.24), channel_id=1, source_target_pairs={{0,16},{8,24},{16,0},{24,8},{1,17},{9,25},{17,1},{25,9},{2,18},{10... | collective-permute-start | bytes 20 | tf_op jit(solution)/shard_map/ppermute | solution.py:21
  39.9 1.3 collective-permute-start.6
  41.2 17.4 %collective-permute-start.8 = (f32[384,384]{1,0:T(8,128)}, f32[384,384]{1,0:T(8,128)S(1)}, u32[]{:S(2)}, u32[]{:S(2)}) collective-permute-start(f32[384,384]{1,0:T(8,128)} %copy-done.28), channel_id=1, source_target_pairs={{0,1},{1,2},{2,3},{3,0},{4,5},{5,6},{6,7},{7,4},{8,9},{9,10},{10,1... | collective-permute-start | bytes 1769480 | tf_op jit(solution)/shard_map/ppermute | solution.py:21
  45.2 15.7 %copy-start.4 = (bf16[7,384,384]{2,1,0:T(8,128)(2,1)S(1)}, bf16[7,384,384]{2,1,0:T(8,128)(2,1)}, u32[]{:S(2)}) copy-start(bf16[7,384,384]{2,1,0:T(8,128)(2,1)} %copy-done.3) | copy-start | bytes 6193156
  45.9 24.8 %collective-permute-start.20 = (f32[392,384]{1,0:T(8,128)S(1)}, f32[392,384]{1,0:T(8,128)S(1)}, u32[]{:S(2)}, u32[]{:S(2)}) collective-permute-start(f32[392,384]{1,0:T(8,128)S(1)} %pick_own.1), channel_id=1, source_target_pairs={{0,24},{8,0},{16,8},{24,16},{1,25},{9,1},{17,9},{25,17},{2,26},{10... | collective-permute-start | bytes 1806344 | tf_op jit(solution)/shard_map/ppermute | solution.py:21
  47.3 25.0 %collective-permute-start.21 = (f32[392,384]{1,0:T(8,128)S(1)}, f32[392,384]{1,0:T(8,128)S(1)}, u32[]{:S(2)}, u32[]{:S(2)}) collective-permute-start(f32[392,384]{1,0:T(8,128)S(1)} %pick_own.1), channel_id=1, source_target_pairs={{0,8},{8,16},{16,24},{24,0},{1,9},{9,17},{17,25},{25,1},{2,10},{10... | collective-permute-start | bytes 1806344 | tf_op jit(solution)/shard_map/ppermute | solution.py:21
  47.3 25.8 %collective-permute-start.17 = (f32[392,384]{1,0:T(8,128)S(1)}, f32[392,384]{1,0:T(8,128)S(1)}, u32[]{:S(2)}, u32[]{:S(2)}) collective-permute-start(f32[392,384]{1,0:T(8,128)S(1)} %pick_own.1), channel_id=1, source_target_pairs={{0,4},{4,0},{1,5},{5,1},{2,6},{6,2},{3,7},{7,3},{8,12},{12,8},{9,1... | collective-permute-start | bytes 1806344 | tf_op jit(solution)/shard_map/ppermute | solution.py:21
  58.6 16.9 %collective-permute-start.14 = (f32[392,384]{1,0:T(8,128)S(1)}, f32[392,384]{1,0:T(8,128)S(1)}, u32[]{:S(2)}, u32[]{:S(2)}) collective-permute-start(f32[392,384]{1,0:T(8,128)S(1)} %pick_own.1), channel_id=1, source_target_pairs={{0,3},{1,0},{2,1},{3,2},{4,7},{5,4},{6,5},{7,6},{8,11},{9,8},{10,9... | collective-permute-start | bytes 1806344 | tf_op jit(solution)/shard_map/ppermute | solution.py:21
  60.9 27.8 %collective-permute-start.15 = (f32[392,384]{1,0:T(8,128)S(1)}, f32[392,384]{1,0:T(8,128)S(1)}, u32[]{:S(2)}, u32[]{:S(2)}) collective-permute-start(f32[392,384]{1,0:T(8,128)S(1)} %pick_own.1), channel_id=1, source_target_pairs={{0,1},{1,2},{2,3},{3,0},{4,5},{5,6},{6,7},{7,4},{8,9},{9,10},{10,1... | collective-permute-start | bytes 1806344 | tf_op jit(solution)/shard_map/ppermute | solution.py:21
  71.5 47.9 %collective-permute-start.18 = (f32[384,384]{1,0:T(8,128)}, f32[384,384]{1,0:T(8,128)}, u32[]{:S(2)}, u32[]{:S(2)}) collective-permute-start(f32[384,384]{1,0:T(8,128)} %get-tuple-element.32.square_ref), channel_id=1, source_target_pairs={{0,24},{8,0},{16,8},{24,16},{1,25},{9,1},{17,9},{25,17},{2,26},{10... | collective-permute-start | bytes 1769480 | tf_op jit(solution)/shard_map/ppermute | solution.py:21
  73.1 46.3 %collective-permute-start.19 = (f32[384,384]{1,0:T(8,128)}, f32[384,384]{1,0:T(8,128)}, u32[]{:S(2)}, u32[]{:S(2)}) collective-permute-start(f32[384,384]{1,0:T(8,128)} %get-tuple-element.32.square_ref), channel_id=1, source_target_pairs={{0,8},{8,16},{16,24},{24,0},{1,9},{9,17},{17,25},{25,1},{2,10},{10... | collective-permute-start | bytes 1769480 | tf_op jit(solution)/shard_map/ppermute | solution.py:21
  73.9 49.4 %collective-permute-start.16 = (f32[384,384]{1,0:T(8,128)}, f32[384,384]{1,0:T(8,128)}, u32[]{:S(2)}, u32[]{:S(2)}) collective-permute-start(f32[384,384]{1,0:T(8,128)} %get-tuple-element.32.square_ref), channel_id=1, source_target_pairs={{0,4},{4,0},{1,5},{5,1},{2,6},{6,2},{3,7},{7,3},{8,12},{12,8},{9,1... | collective-permute-start | bytes 1769480 | tf_op jit(solution)/shard_map/ppermute | solution.py:21
  76.3 50.8 %collective-permute-start.12 = (f32[384,384]{1,0:T(8,128)}, f32[384,384]{1,0:T(8,128)}, u32[]{:S(2)}, u32[]{:S(2)}) collective-permute-start(f32[384,384]{1,0:T(8,128)} %get-tuple-element.32.square_ref), channel_id=1, source_target_pairs={{0,3},{1,0},{2,1},{3,2},{4,7},{5,4},{6,5},{7,6},{8,11},{9,8},{10,9... | collective-permute-start | bytes 1769480 | tf_op jit(solution)/shard_map/ppermute | solution.py:21
  89.5 37.6 %collective-permute-start.13 = (f32[384,384]{1,0:T(8,128)}, f32[384,384]{1,0:T(8,128)}, u32[]{:S(2)}, u32[]{:S(2)}) collective-permute-start(f32[384,384]{1,0:T(8,128)} %get-tuple-element.32.square_ref), channel_id=1, source_target_pairs={{0,1},{1,2},{2,3},{3,0},{4,5},{5,6},{6,7},{7,4},{8,9},{9,10},{10,1... | collective-permute-start | bytes 1769480 | tf_op jit(solution)/shard_map/ppermute | solution.py:21
  (28 other events, 73.5 us)
where the time goes:
time: 132 us; the launch traced here: 131 us
  Pallas kernels  47.7 us (36%)
  starting transfers between devices  34.4 us (26%)
  waiting for transfers between devices  21.8 us (17%)
  local copies, waits for them, and re-layouts  21.5 us (16%)
  between operations  5.42 us (4%)
    ppermute x22, starting transfers between devices, passed_along(): return lax.ppermute(value, axis, pairs)  34.4 us
    ppermute x22, waiting for transfers between devices, passed_along(): return lax.ppermute(value, axis, pairs)  21.8 us
    unnamed x60, local copies, waits for them, and re-layouts  21.5 us
    pallas_call x3, Pallas kernels, cube_parts(): pl.pallas_call(kernel, in_specs=[SMEM] + [VMEM] * 8, out_specs=[VMEM] * 3...  14.9 us
    pallas_call x3, Pallas kernels, pair_output(): pl.pallas_call(kernel, grid=(2,), in_specs=[SMEM, SMEM, VMEM, VMEM, block...  11.5 us
    pallas_call x3, Pallas kernels, side_products(): pl.pallas_call(kernel, in_specs=[VMEM] * len(operands), out_specs=[VMEM]...  6.94 us
    pallas_call x1, Pallas kernels, first_products(): pl.pallas_call(first_kernel, grid=(slots,), in_specs=[pl.BlockSpec((1, wi...  6.91 us
    pallas_call x3, Pallas kernels, pick_pair(): pl.pallas_call(kernel, in_specs=[HBM], out_specs=[VMEM] * len(shapes), ou...  2.84 us
  transfers between devices with their start and end apart: 22, of which 5 were waited for; matrix products, arithmetic and copies ran while one was open for 0% of the time, Pallas kernels for 33%

commit v1 on v0

--- a/solution.py
+++ b/solution.py
@@ -38,11 +38,9 @@
     return (passed_along(block, axis, -1), passed_along(block, axis, 1))
 
 
-def summed_over(value, axis):
-    total = value
-    for step in range(1, lax.axis_size(axis)):
-        total = total + passed_along(value, axis, step)
-    return total
+def all_along(value, axis):
+    steps = range(1, lax.axis_size(axis))
+    return [value] + [passed_along(value, axis, k) for k in steps]
 
 
 HBM = pl.BlockSpec(memory_space=pltpu.HBM)
@@ -60,11 +58,35 @@
     return high, (value - high.astype(WORD)).astype(HALF)
 
 
+def dot(left, right):
+    return jnp.dot(left, right, preferred_element_type=WORD)
+
+
+def beside(*values):
+    return jnp.concatenate(values, axis=1)
+
+
+def below(*values):
+    return jnp.concatenate(values, axis=0)
+
+
 def dot3(left, right):
-    def dot(a, b):
-        return jnp.dot(a, b, preferred_element_type=WORD)
-
-    return dot(left[0], right[0]) + (dot(left[0], right[1]) + dot(left[1], right[0]))
+    width = right[0].shape[1]
+    wide = dot(left[0], beside(*right))
+    return (wide[:, width:] + dot(left[1], right[0])) + wide[:, :width]
+
+
+def dot3_sum(lefts, rights):
+    left = [beside(*(pair[part] for pair in lefts)) for part in (0, 1)]
+    right = [below(*(pair[part] for pair in rights)) for part in (0, 1)]
+    return dot3(left, right)
+
+
+def dot3_wide(left, rights):
+    high, low = (beside(*(pair[part] for pair in rights)) for part in (0, 1))
+    wide = dot(beside(*left), below(high, high)) + dot(left[0], low)
+    width = wide.shape[1] // len(rights)
+    return [wide[:, i * width : (i + 1) * width] for i in range(len(rights))]
 
 
 def both(pair, s):
@@ -196,7 +218,7 @@
     width = halves[0].shape[-1]
 
     def kernel(keep_ref, high, low, f0, f1, p0, p1, products, side, pair, near, mix):
-        nears, mixes = [], []
+        squares, nears, values, mixes = [], [], [], []
         for index, (face, ref, (_, part)) in enumerate(
             zip((f0, f1), (p0, p1), partners)
         ):
@@ -205,11 +227,12 @@
             kept = face[back : back + 1, :]
             value = ref[...] if part is None else ref[part]
             coupled = dot3(both((high, low), s), split(face[:width] * SCALE))
-            square = keep_ref[s].astype(WORD) * (products[s] + coupled)
-            pair[index] = dot3(both((high, low), 0), split(square))
-            nears.append(dot3(split(kept * coupled), split(value * SCALE)))
+            squares.append(split(keep_ref[s].astype(WORD) * (products[s] + coupled)))
+            nears.append(split(kept * coupled))
+            values.append(split(value * SCALE))
             mixes.append(kept * side[index])
-        near[...] = nears[0] + nears[1]
+        pair[0], pair[1] = dot3_wide(both((high, low), 0), squares)
+        near[...] = dot3_sum(nears, values)
         mix[...] = mixes[0] + mixes[1]
 
     return pl.pallas_call(
@@ -236,7 +259,7 @@
         for ref in refs[3::2]:
             mix = mix + ref[...]
         own = both((high, low), 0)
-        out[...] = dot3(own, split(square_ref[...])) + (dot3(split(mix), own) + near)
+        out[...] = near + dot3_sum((own, split(mix)), (split(square_ref[...]), own))
 
     return pl.pallas_call(
         kernel,
@@ -248,52 +271,84 @@
     )(*halves, square, *parts)
 
 
-def weighted(scalars, keep, raw, cube):
-    small = scalars[1]
+def total_of(sums):
+    def kernel(*refs):
+        *parts, out = refs
+        total = parts[0][0]
+        for part in parts[1:]:
+            total = total + part[0]
+        out[0] = total
+
+    return pl.pallas_call(
+        kernel,
+        in_specs=[SMEM] * len(sums),
+        out_specs=SMEM,
+        out_shape=struct(1),
+        compiler_params=PARAMS,
+        name="total_of",
+    )(*sums)
+
+
+def weighted(norm_refs, entry_count, keep, raw, cube):
+    norm_sq = norm_refs[0][0]
+    for ref in norm_refs[1:]:
+        norm_sq = norm_sq + ref[0]
+    row = jnp.full((1, raw.shape[-1]), norm_sq, WORD)
+    factor = TARGET_RMS / jnp.sqrt(row / entry_count)
+    small = factor * (1.0 / SCALE)
     kept = keep.astype(WORD)
-    return kept * ((1.5 * scalars[0]) * raw - 0.5 * (((cube * small) * small) * small))
-
-
-def own_output(scalars, keep, raw, cube):
+    return kept * ((1.5 * factor) * raw - 0.5 * (((cube * small) * small) * small))
+
+
+def own_output(norms, entry_count, keep, raw, cube):
     width = raw.shape[-1]
     block = pl.BlockSpec((1, width, width), lambda i: (0, 0, 0))
-
-    def kernel(scalars, keep_ref, raw_ref, cube_ref, out):
-        out[0] = weighted(scalars, keep_ref[0], raw_ref[0], cube_ref[...])
+    count = len(norms)
+
+    def kernel(*refs):
+        keep_ref, raw_ref, cube_ref, out = refs[count:]
+        out[0] = weighted(
+            refs[:count], entry_count, keep_ref[0], raw_ref[0], cube_ref[...]
+        )
 
     return pl.pallas_call(
         kernel,
         grid=(1,),
-        in_specs=[SMEM, SMEM, block, VMEM],
+        in_specs=[SMEM] * count + [SMEM, block, VMEM],
         out_specs=block,
         out_shape=struct(*raw.shape),
         compiler_params=PARAMS,
         name="own_output",
-    )(scalars, keep, raw, cube)
-
-
-def pair_output(scalars, keep, halves, raw, slot, square_faces, part, out):
+    )(*norms, keep, raw, cube)
+
+
+def pair_output(norms, entry_count, keep, halves, raw, slot, square_faces, part, out):
     width = raw.shape[-1]
     block = pl.BlockSpec((1, width, width), lambda i: (slot + i, 0, 0))
-
-    def kernel(scalars, keep_ref, high, low, raw_ref, f0, f1, part_ref, _, out_ref):
+    count = len(norms)
+
+    def kernel(*refs):
+        keep_ref, high, low, raw_ref, f0, f1, part_ref, _, out_ref = refs[count:]
         for index, face in enumerate((f0, f1)):
 
             @pl.when(pl.program_id(0) == index)
             def _(index=index, face=face):
                 s = slot + index
                 cube = part_ref[index] + dot3(both((high, low), s), split(face[...]))
-                out_ref[0] = weighted(scalars, keep_ref[s], raw_ref[0], cube)
+                out_ref[0] = weighted(
+                    refs[:count], entry_count, keep_ref[s], raw_ref[0], cube
+                )
 
     return pl.pallas_call(
         kernel,
         grid=(2,),
-        in_specs=[SMEM, SMEM, VMEM, VMEM, block, VMEM, VMEM, VMEM, HBM],
+        in_specs=[SMEM] * count
+        + [SMEM, VMEM, VMEM, block, VMEM, VMEM, VMEM, HBM],
         out_specs=block,
         out_shape=struct(*raw.shape),
-        input_output_aliases={8: 0},
-        compiler_params=PARAMS,
-    )(scalars, keep, *halves, raw, *square_faces, part, out)
+        input_output_aliases={count + 7: 0},
+        compiler_params=PARAMS,
+    )(*norms, keep, *halves, raw, *square_faces, part, out)
 
 
 def body(hamiltonian, keep_mask):
@@ -315,11 +370,11 @@
 
     high, low, products, squares = first_products(raw)
     halves = (high, low)
-    norm_sq = squares[0]
+    norms = [squares]
     for axis, _ in SIDES:
-        norm_sq = summed_over(norm_sq, axis)
-    factor = TARGET_RMS / jnp.sqrt(norm_sq / entry_count)
-    scalars = jnp.stack([factor, factor * (1.0 / SCALE)])
+        if len(norms) > 1:
+            norms = [total_of(norms)]
+        norms = all_along(norms[0], axis)
 
     for axis, slot in LOCAL_ORDER[:-1]:
         (side[slot],) = side_products(halves, slot, partners[slot])
@@ -337,10 +392,18 @@
         )
         sums += [near, mix]
     cube = own_cube(halves, square, sums)
-    out = own_output(scalars, keep, raw, cube)
+    out = own_output(norms, entry_count, keep, raw, cube)
     for axis, slot in LOCAL_ORDER:
         out = pair_output(
-            scalars, keep, halves, raw, slot, square_faces[slot], parts[slot], out
+            norms,
+            entry_count,
+            keep,
+            halves,
+            raw,
+            slot,
+            square_faces[slot],
+            parts[slot],
+            out,
         )
     return out
 

time: 132 us -> 123 us (0.932)
  waiting for transfers between devices: 21.8 us -> 42.6 us
  local copies, waits for them, and re-layouts: 21.5 us -> 2.18 us
  between operations: 5.42 us -> 0.19 us
  starting transfers between devices: 34.4 us -> 29.2 us
    ppermute x22, waiting for transfers between devices: 21.8 us -> 42.6 us  [passed_along(): return lax.ppermute(value, axis, pairs)]
    unnamed x60 -> x6, local copies, waits for them, and re-layouts: 21.5 us -> 2.18 us
    pallas_call x4 -> x6, Pallas kernels: 13 us -> 25.5 us  [the longest x3 16.7 us: pair_output(): pl.pallas_call(kernel, grid=(2,), in_specs=[SMEM] * count + [SMEM, VMEM,...]
    ppermute x22, starting transfers between devices: 34.4 us -> 29.2 us  [passed_along(): return lax.ppermute(value, axis, pairs)]
    pallas_call x3, Pallas kernels: 14.9 us -> 10.5 us  [cube_parts(): pl.pallas_call(kernel, in_specs=[SMEM] + [VMEM] * 8, out_specs=[VMEM] * 3...]
    pallas_call x3, Pallas kernels: 6.94 us -> 3.6 us  [side_products(): pl.pallas_call(kernel, in_specs=[VMEM] * len(operands), out_specs=[VMEM]...]
    pallas_call x3, Pallas kernels: 2.84 us -> 0.76 us  [pick_pair(): pl.pallas_call(kernel, in_specs=[HBM], out_specs=[VMEM] * len(shapes), ou...]
    pallas_call x1, Pallas kernels: 2.53 us -> 1.05 us  [own_cube(): pl.pallas_call(kernel, in_specs=[VMEM] * (3 + len(parts)), out_specs=VMEM...]
  transfers between devices with their start and end apart: 22 -> 22, of which waited for: 5 -> 7; matrix products, arithmetic and copies ran while one was open for 0% -> 0% of each run, Pallas kernels for 33% -> 35%
where the time goes in v1:
time: 123 us
  Pallas kernels  48.5 us (39%)
  waiting for transfers between devices  42.6 us (35%)
  starting transfers between devices  29.2 us (24%)
  local copies, waits for them, and re-layouts  2.18 us (2%)
    ppermute x22, waiting for transfers between devices, passed_along(): return lax.ppermute(value, axis, pairs)  42.6 us
    ppermute x22, starting transfers between devices, passed_along(): return lax.ppermute(value, axis, pairs)  29.2 us
    pallas_call x3, Pallas kernels, pair_output(): pl.pallas_call(kernel, grid=(2,), in_specs=[SMEM] * count + [SMEM, VMEM,...  16.7 us
    pallas_call x3, Pallas kernels, cube_parts(): pl.pallas_call(kernel, in_specs=[SMEM] + [VMEM] * 8, out_specs=[VMEM] * 3...  10.5 us
    pallas_call x1, Pallas kernels, first_products(): pl.pallas_call(first_kernel, grid=(slots,), in_specs=[pl.BlockSpec((1, wi...  6.39 us
    pallas_call x2, Pallas kernels, total_of(): pl.pallas_call(kernel, in_specs=[SMEM] * len(sums), out_specs=SMEM, out_s...  4.81 us
    pallas_call x1, Pallas kernels, own_output(): pl.pallas_call(kernel, grid=(1,), in_specs=[SMEM] * count + [SMEM, block,...  4.02 us
    pallas_call x3, Pallas kernels, side_products(): pl.pallas_call(kernel, in_specs=[VMEM] * len(operands), out_specs=[VMEM]...  3.6 us
  transfers between devices with their start and end apart: 22, of which 7 were waited for; matrix products, arithmetic and copies ran while one was open for 0% of the time, Pallas kernels for 35%

profile of v1, /device:TPU:0, one launch (start us, length us, event | category | flops | bytes accessed | tf_op | source)
XLA Modules:
  0.0 122.7 jit_solution(7017412288041118800)
XLA Ops:
  0.0 2.2 %copy-done = f32[1,1,1,7,384,384]{5,4,3,2,1,0:T(8,128)S(1)} copy-done((f32[1,1,1,7,384,384]{5,4,3,2,1,0:T(8,128)S(1)}, f32[1,1,1,7,384,384]{5,4,3,2,1,0:T(8,128)}, u32[]{:S(2)}) %copy-start) | copy-done | bytes 4128792
  2.4 3.1 %collective-permute-start.11 = (f32[2,384,384]{2,1,0:T(8,128)S(1)}, f32[2,384,384]{2,1,0:T(8,128)S(1)}, u32[]{:S(2)}, u32[]{:S(2)}) collective-permute-start(f32[2,384,384]{2,1,0:T(8,128)S(1)} %shard_map.31), channel_id=1, source_target_pairs={{0,4},{4,0},{1,5},{5,1},{2,6},{6,2},{3,7},{7,3},{8,12},{12,8},{9,1... | collective-permute-start | bytes 3538952 | tf_op jit(solution)/shard_map/ppermute | solution.py:21
  5.5 6.4 %first_products.1 = (bf16[7,384,384]{2,1,0:T(8,128)(2,1)S(1)}, bf16[7,384,384]{2,1,0:T(8,128)(2,1)S(1)}, f32[7,384,384]{2,1,0:T(8,128)S(1)}, f32[1]{0:T(128)}) custom-call(f32[7,384,384]{2,1,0:T(8,128)S(1)} %bitcast.4), custom_call_target="tpu_custom_call" | custom-call | tf_op jit(solution)/shard_map/first_products/pallas_call | solution.py:167
  13.5 2.6 %collective-permute-start.1 = (f32[1]{0:T(128)}, f32[1]{0:T(128)}, u32[]{:S(2)}, u32[]{:S(2)}) collective-permute-start(f32[1]{0:T(128)} %get-tuple-element.24.refs_0_), channel_id=1, source_target_pairs={{0,2},{1,3},{2,0},{3,1},{4,6},{5,7},{6,4},{7,5},{8,10},{9,11},{10,... | collective-permute-start | bytes 20 | tf_op jit(solution)/shard_map/ppermute | solution.py:21
  18.1 1.8 %collective-permute-start.9 = (f32[384,384]{1,0:T(8,128)S(1)}, f32[384,384]{1,0:T(8,128)S(1)}, u32[]{:S(2)}, u32[]{:S(2)}) collective-permute-start(f32[384,384]{1,0:T(8,128)S(1)} %get-tuple-element.30), channel_id=1, source_target_pairs={{0,24},{8,0},{16,8},{24,16},{1,25},{9,1},{17,9},{25,17},{2,26},{10... | collective-permute-start | bytes 1769480 | tf_op jit(solution)/shard_map/ppermute | solution.py:21
  20.3 3.0 %total_of.2.refs_0_ = f32[1]{0:T(128)} custom-call(f32[1]{0:T(128)} %get-tuple-element.24.refs_0_, f32[1]{0:T(128)} %collective-permute-done.refs_1_, f32[1]{0:T(128)} %collective-permute-done.1.refs_2_, f32[1]{0:T(128)} %collective-permute-done.2.refs_3_), custom_call_target="tpu_custom_call" | custom-call | tf_op jit(solution)/shard_map/total_of/pallas_call | solution.py:282
  23.9 7.6 %collective-permute-done.3.refs_1_ = f32[1]{0:T(128)} collective-permute-done((f32[1]{0:T(128)}, f32[1]{0:T(128)}, u32[]{:S(2)}, u32[]{:S(2)}) %collective-permute-start.3) | collective-permute-done | bytes 36 | tf_op jit(solution)/shard_map/ppermute | solution.py:21
  31.5 1.8 %total_of.3.refs_0_ = f32[1]{0:T(128)} custom-call(f32[1]{0:T(128)} %total_of.2.refs_0_, f32[1]{0:T(128)} %collective-permute-done.3.refs_1_), custom_call_target="tpu_custom_call" | custom-call | tf_op jit(solution)/shard_map/total_of/pallas_call | solution.py:282
  33.4 3.0 %collective-permute-done.4.refs_1_ = f32[1]{0:T(128)} collective-permute-done((f32[1]{0:T(128)}, f32[1]{0:T(128)}, u32[]{:S(2)}, u32[]{:S(2)}) %collective-permute-start.4) | collective-permute-done | bytes 36 | tf_op jit(solution)/shard_map/ppermute | solution.py:21
  36.4 1.7 %collective-permute-start.5 = (f32[1]{0:T(128)}, f32[1]{0:T(128)}, u32[]{:S(2)}, u32[]{:S(2)}) collective-permute-start(f32[1]{0:T(128)} %total_of.3.refs_0_), channel_id=1, source_target_pairs={{0,16},{8,24},{16,0},{24,8},{1,17},{9,25},{17,1},{25,9},{2,18},{10... | collective-permute-start | bytes 20 | tf_op jit(solution)/shard_map/ppermute | solution.py:21
  38.1 2.0 %collective-permute-done.5.refs_2_ = f32[1]{0:T(128)} collective-permute-done((f32[1]{0:T(128)}, f32[1]{0:T(128)}, u32[]{:S(2)}, u32[]{:S(2)}) %collective-permute-start.5) | collective-permute-done | bytes 36 | tf_op jit(solution)/shard_map/ppermute | solution.py:21
  41.6 1.8 %collective-permute-start.8 = (f32[384,384]{1,0:T(8,128)S(1)}, f32[384,384]{1,0:T(8,128)S(1)}, u32[]{:S(2)}, u32[]{:S(2)}) collective-permute-start(f32[384,384]{1,0:T(8,128)S(1)} %get-tuple-element.28), channel_id=1, source_target_pairs={{0,1},{1,2},{2,3},{3,0},{4,5},{5,6},{6,7},{7,4},{8,9},{9,10},{10,1... | collective-permute-start | bytes 1769480 | tf_op jit(solution)/shard_map/ppermute | solution.py:21
  47.3 11.4 %collective-permute-done.8.second.p1 = f32[384,384]{1,0:T(8,128)S(1)} collective-permute-done((f32[384,384]{1,0:T(8,128)S(1)}, f32[384,384]{1,0:T(8,128)S(1)}, u32[]{:S(2)}, u32[]{:S(2)}) %collective-permute-start.8) | collective-permute-done | bytes 589856 | tf_op jit(solution)/shard_map/ppermute | solution.py:21
  58.7 2.3 %collective-permute-start.14 = (f32[392,384]{1,0:T(8,128)S(1)}, f32[392,384]{1,0:T(8,128)S(1)}, u32[]{:S(2)}, u32[]{:S(2)}) collective-permute-start(f32[392,384]{1,0:T(8,128)S(1)} %pick_own.1), channel_id=1, source_target_pairs={{0,3},{1,0},{2,1},{3,2},{4,7},{5,4},{6,5},{7,6},{8,11},{9,8},{10,9... | collective-permute-start | bytes 1806344 | tf_op jit(solution)/shard_map/ppermute | solution.py:21
  67.4 7.6 %collective-permute-done.14.f0 = f32[392,384]{1,0:T(8,128)S(1)} collective-permute-done((f32[392,384]{1,0:T(8,128)S(1)}, f32[392,384]{1,0:T(8,128)S(1)}, u32[]{:S(2)}, u32[]{:S(2)}) %collective-permute-start.14) | collective-permute-done | bytes 602144 | tf_op jit(solution)/shard_map/ppermute | solution.py:21
  75.0 4.3 %collective-permute-start.12 = (f32[384,384]{1,0:T(8,128)S(1)}, f32[384,384]{1,0:T(8,128)S(1)}, u32[]{:S(2)}, u32[]{:S(2)}) collective-permute-start(f32[384,384]{1,0:T(8,128)S(1)} %get-tuple-element.32.square_ref), channel_id=1, source_target_pairs={{0,3},{1,0},{2,1},{3,2},{4,7},{5,4},{6,5},{7,6},{8,11},{9,8},{10,9... | collective-permute-start | bytes 1769480 | tf_op jit(solution)/shard_map/ppermute | solution.py:21
  79.3 9.5 %collective-permute-done.15.f1 = f32[392,384]{1,0:T(8,128)S(1)} collective-permute-done((f32[392,384]{1,0:T(8,128)S(1)}, f32[392,384]{1,0:T(8,128)S(1)}, u32[]{:S(2)}, u32[]{:S(2)}) %collective-permute-start.15) | collective-permute-done | bytes 602144 | tf_op jit(solution)/shard_map/ppermute | solution.py:21
  90.4 3.5 %shard_map.36 = (f32[2,384,384]{2,1,0:T(8,128)S(1)}, f32[384,384]{1,0:T(8,128)S(1)}, f32[384,384]{1,0:T(8,128)S(1)}) custom-call(s32[7]{0:T(128)S(1)} %bitcast.13, bf16[7,384,384]{2,1,0:T(8,128)(2,1)S(1)} %get-tuple-element.25.high.refs_5_, bf16[7,384,384]{2,1,0:T(8,128)(2,1)S(1)} %get-tuple-element.26.low.refs_6_, ...), custom_call_target="tpu_custom_call" | custom-call | tf_op jit(solution)/shard_map/pallas_call | solution.py:238
  93.9 3.5 %shard_map.35 = (f32[2,384,384]{2,1,0:T(8,128)S(1)}, f32[384,384]{1,0:T(8,128)S(1)}, f32[384,384]{1,0:T(8,128)S(1)}) custom-call(s32[7]{0:T(128)S(1)} %bitcast.14, bf16[7,384,384]{2,1,0:T(8,128)(2,1)S(1)} %get-tuple-element.25.high.refs_5_, bf16[7,384,384]{2,1,0:T(8,128)(2,1)S(1)} %get-tuple-element.26.low.refs_6_, ...), custom_call_target="tpu_custom_call" | custom-call | tf_op jit(solution)/shard_map/pallas_call | solution.py:238
  97.4 3.5 %shard_map.34 = (f32[2,384,384]{2,1,0:T(8,128)S(1)}, f32[384,384]{1,0:T(8,128)S(1)}, f32[384,384]{1,0:T(8,128)S(1)}) custom-call(s32[7]{0:T(128)S(1)} %bitcast.15, bf16[7,384,384]{2,1,0:T(8,128)(2,1)S(1)} %get-tuple-element.25.high.refs_5_, bf16[7,384,384]{2,1,0:T(8,128)(2,1)S(1)} %get-tuple-element.26.low.refs_6_, ...), custom_call_target="tpu_custom_call" | custom-call | tf_op jit(solution)/shard_map/pallas_call | solution.py:238
  102.0 4.0 %own_output.1.refs_11_ = f32[7,384,384]{2,1,0:T(8,128)} custom-call(f32[1]{0:T(128)} %total_of.3.refs_0_, f32[1]{0:T(128)} %collective-permute-done.4.refs_1_, f32[1]{0:T(128)} %collective-permute-done.5.refs_2_, f32[1]{0:T(128)} %collective-permute-done.6.refs_3_, s32[7]{0:T(128)S(1)} %bitcast.16, f32[7,384,384]{2,1,0:T(8,128)S(1)} %bitcast.8, ...), custom_call_target="tpu_custom_call" | custom-call | tf_op jit(solution)/shard_map/own_output/pallas_call | solution.py:314
  106.0 5.7 %shard_map.37.refs_11_ = f32[7,384,384]{2,1,0:T(8,128)} custom-call(f32[1]{0:T(128)} %total_of.3.refs_0_, f32[1]{0:T(128)} %collective-permute-done.4.refs_1_, f32[1]{0:T(128)} %collective-permute-done.5.refs_2_, f32[1]{0:T(128)} %collective-permute-done.6.refs_3_, s32[7]{0:T(128)S(1)} %bitcast.17, ...), custom_call_target="tpu_custom_call", output_to_operand_aliasing={{}: (11, {})} | custom-call | tf_op jit(solution)/shard_map/pallas_call | solution.py:342
  111.7 5.5 %shard_map.38.refs_11_ = f32[7,384,384]{2,1,0:T(8,128)} custom-call(f32[1]{0:T(128)} %total_of.3.refs_0_, f32[1]{0:T(128)} %collective-permute-done.4.refs_1_, f32[1]{0:T(128)} %collective-permute-done.5.refs_2_, f32[1]{0:T(128)} %collective-permute-done.6.refs_3_, s32[7]{0:T(128)S(1)} %bitcast.18, ...), custom_call_target="tpu_custom_call", output_to_operand_aliasing={{}: (11, {})} | custom-call | tf_op jit(solution)/shard_map/pallas_call | solution.py:342
  117.2 5.5 %shard_map.39 = f32[7,384,384]{2,1,0:T(8,128)} custom-call(f32[1]{0:T(128)} %total_of.3.refs_0_, f32[1]{0:T(128)} %collective-permute-done.4.refs_1_, f32[1]{0:T(128)} %collective-permute-done.5.refs_2_, f32[1]{0:T(128)} %collective-permute-done.6.refs_3_, s32[7]{0:T(128)S(1)} %bitcast.19, ...), custom_call_target="tpu_custom_call", output_to_operand_aliasing={{}: (11, {})} | custom-call | tf_op jit(solution)/shard_map/pallas_call | solution.py:342
  (44 shorter events, 19.3 us)
Async XLA Ops:
  2.4 58.6 %collective-permute-start.11 = (f32[2,384,384]{2,1,0:T(8,128)S(1)}, f32[2,384,384]{2,1,0:T(8,128)S(1)}, u32[]{:S(2)}, u32[]{:S(2)}) collective-permute-start(f32[2,384,384]{2,1,0:T(8,128)S(1)} %shard_map.31), channel_id=1, source_target_pairs={{0,4},{4,0},{1,5},{5,1},{2,6},{6,2},{3,7},{7,3},{8,12},{12,8},{9,1... | collective-permute-start | bytes 3538952 | tf_op jit(solution)/shard_map/ppermute | solution.py:21
  11.9 6.2 %collective-permute-start = (f32[1]{0:T(128)}, f32[1]{0:T(128)}, u32[]{:S(2)}, u32[]{:S(2)}) collective-permute-start(f32[1]{0:T(128)} %get-tuple-element.24.refs_0_), channel_id=1, source_target_pairs={{0,1},{1,2},{2,3},{3,0},{4,5},{5,6},{6,7},{7,4},{8,9},{9,10},{10,1... | collective-permute-start | bytes 20 | tf_op jit(solution)/shard_map/ppermute | solution.py:21
  13.5 6.4 %collective-permute-start.1 = (f32[1]{0:T(128)}, f32[1]{0:T(128)}, u32[]{:S(2)}, u32[]{:S(2)}) collective-permute-start(f32[1]{0:T(128)} %get-tuple-element.24.refs_0_), channel_id=1, source_target_pairs={{0,2},{1,3},{2,0},{3,1},{4,6},{5,7},{6,4},{7,5},{8,10},{9,11},{10,... | collective-permute-start | bytes 20 | tf_op jit(solution)/shard_map/ppermute | solution.py:21
  16.1 4.2 %collective-permute-start.2 = (f32[1]{0:T(128)}, f32[1]{0:T(128)}, u32[]{:S(2)}, u32[]{:S(2)}) collective-permute-start(f32[1]{0:T(128)} %get-tuple-element.24.refs_0_), channel_id=1, source_target_pairs={{0,3},{1,0},{2,1},{3,2},{4,7},{5,4},{6,5},{7,6},{8,11},{9,8},{10,9... | collective-permute-start | bytes 20 | tf_op jit(solution)/shard_map/ppermute | solution.py:21
  17.7 25.7 %copy-start.1 = (f32[1,1,1,7,384,384]{5,4,3,2,1,0:T(8,128)S(1)}, f32[1,1,1,7,384,384]{5,4,3,2,1,0:T(8,128)}, u32[]{:S(2)}) copy-start(f32[1,1,1,7,384,384]{5,4,3,2,1,0:T(8,128)} %param.2) | copy-start | bytes 12386308
  17.7 25.7 %copy-start.2 = (s32[1,1,1,7]{3,2,1,0:T(1,128)S(1)}, s32[1,1,1,7]{3,2,1,0:T(1,128)}, u32[]{:S(2)}) copy-start(s32[1,1,1,7]{3,2,1,0:T(1,128)} %param.3) | copy-start | bytes 88
  17.7 26.4 %collective-permute-start.10 = (f32[384,384]{1,0:T(8,128)S(1)}, f32[384,384]{1,0:T(8,128)S(1)}, u32[]{:S(2)}, u32[]{:S(2)}) collective-permute-start(f32[384,384]{1,0:T(8,128)S(1)} %get-tuple-element.31), channel_id=1, source_target_pairs={{0,8},{8,16},{16,24},{24,0},{1,9},{9,17},{17,25},{25,1},{2,10},{10... | collective-permute-start | bytes 1769480 | tf_op jit(solution)/shard_map/ppermute | solution.py:21
  18.1 27.6 %collective-permute-start.9 = (f32[384,384]{1,0:T(8,128)S(1)}, f32[384,384]{1,0:T(8,128)S(1)}, u32[]{:S(2)}, u32[]{:S(2)}) collective-permute-start(f32[384,384]{1,0:T(8,128)S(1)} %get-tuple-element.30), channel_id=1, source_target_pairs={{0,24},{8,0},{16,8},{24,16},{1,25},{9,1},{17,9},{25,17},{2,26},{10... | collective-permute-start | bytes 1769480 | tf_op jit(solution)/shard_map/ppermute | solution.py:21
  19.9 25.9 %collective-permute-start.7 = (f32[384,384]{1,0:T(8,128)S(1)}, f32[384,384]{1,0:T(8,128)S(1)}, u32[]{:S(2)}, u32[]{:S(2)}) collective-permute-start(f32[384,384]{1,0:T(8,128)S(1)} %get-tuple-element.27), channel_id=1, source_target_pairs={{0,3},{1,0},{2,1},{3,2},{4,7},{5,4},{6,5},{7,6},{8,11},{9,8},{10,9... | collective-permute-start | bytes 1769480 | tf_op jit(solution)/shard_map/ppermute | solution.py:21
  23.3 8.2 %collective-permute-start.3 = (f32[1]{0:T(128)}, f32[1]{0:T(128)}, u32[]{:S(2)}, u32[]{:S(2)}) collective-permute-start(f32[1]{0:T(128)} %total_of.2.refs_0_), channel_id=1, source_target_pairs={{0,4},{4,0},{1,5},{5,1},{2,6},{6,2},{3,7},{7,3},{8,12},{12,8},{9,1... | collective-permute-start | bytes 20 | tf_op jit(solution)/shard_map/ppermute | solution.py:21
  33.3 3.1 %collective-permute-start.4 = (f32[1]{0:T(128)}, f32[1]{0:T(128)}, u32[]{:S(2)}, u32[]{:S(2)}) collective-permute-start(f32[1]{0:T(128)} %total_of.3.refs_0_), channel_id=1, source_target_pairs={{0,8},{8,16},{16,24},{24,0},{1,9},{9,17},{17,25},{25,1},{2,10},{10... | collective-permute-start | bytes 20 | tf_op jit(solution)/shard_map/ppermute | solution.py:21
  36.4 3.7 %collective-permute-start.5 = (f32[1]{0:T(128)}, f32[1]{0:T(128)}, u32[]{:S(2)}, u32[]{:S(2)}) collective-permute-start(f32[1]{0:T(128)} %total_of.3.refs_0_), channel_id=1, source_target_pairs={{0,16},{8,24},{16,0},{24,8},{1,17},{9,25},{17,1},{25,9},{2,18},{10... | collective-permute-start | bytes 20 | tf_op jit(solution)/shard_map/ppermute | solution.py:21
  40.1 1.5 %collective-permute-start.6 = (f32[1]{0:T(128)}, f32[1]{0:T(128)}, u32[]{:S(2)}, u32[]{:S(2)}) collective-permute-start(f32[1]{0:T(128)} %total_of.3.refs_0_), channel_id=1, source_target_pairs={{0,24},{8,0},{16,8},{24,16},{1,25},{9,1},{17,9},{25,17},{2,26},{10... | collective-permute-start | bytes 20 | tf_op jit(solution)/shard_map/ppermute | solution.py:21
  41.6 17.0 %collective-permute-start.8 = (f32[384,384]{1,0:T(8,128)S(1)}, f32[384,384]{1,0:T(8,128)S(1)}, u32[]{:S(2)}, u32[]{:S(2)}) collective-permute-start(f32[384,384]{1,0:T(8,128)S(1)} %get-tuple-element.28), channel_id=1, source_target_pairs={{0,1},{1,2},{2,3},{3,0},{4,5},{5,6},{6,7},{7,4},{8,9},{9,10},{10,1... | collective-permute-start | bytes 1769480 | tf_op jit(solution)/shard_map/ppermute | solution.py:21
  44.1 20.5 %collective-permute-start.20 = (f32[392,384]{1,0:T(8,128)S(1)}, f32[392,384]{1,0:T(8,128)S(1)}, u32[]{:S(2)}, u32[]{:S(2)}) collective-permute-start(f32[392,384]{1,0:T(8,128)S(1)} %pick_own.1), channel_id=1, source_target_pairs={{0,24},{8,0},{16,8},{24,16},{1,25},{9,1},{17,9},{25,17},{2,26},{10... | collective-permute-start | bytes 1806344 | tf_op jit(solution)/shard_map/ppermute | solution.py:21
  45.7 20.1 %collective-permute-start.21 = (f32[392,384]{1,0:T(8,128)S(1)}, f32[392,384]{1,0:T(8,128)S(1)}, u32[]{:S(2)}, u32[]{:S(2)}) collective-permute-start(f32[392,384]{1,0:T(8,128)S(1)} %pick_own.1), channel_id=1, source_target_pairs={{0,8},{8,16},{16,24},{24,0},{1,9},{9,17},{17,25},{25,1},{2,10},{10... | collective-permute-start | bytes 1806344 | tf_op jit(solution)/shard_map/ppermute | solution.py:21
  45.7 20.1 %collective-permute-start.17 = (f32[392,384]{1,0:T(8,128)S(1)}, f32[392,384]{1,0:T(8,128)S(1)}, u32[]{:S(2)}, u32[]{:S(2)}) collective-permute-start(f32[392,384]{1,0:T(8,128)S(1)} %pick_own.1), channel_id=1, source_target_pairs={{0,4},{4,0},{1,5},{5,1},{2,6},{6,2},{3,7},{7,3},{8,12},{12,8},{9,1... | collective-permute-start | bytes 1806344 | tf_op jit(solution)/shard_map/ppermute | solution.py:21
  58.7 16.3 %collective-permute-start.14 = (f32[392,384]{1,0:T(8,128)S(1)}, f32[392,384]{1,0:T(8,128)S(1)}, u32[]{:S(2)}, u32[]{:S(2)}) collective-permute-start(f32[392,384]{1,0:T(8,128)S(1)} %pick_own.1), channel_id=1, source_target_pairs={{0,3},{1,0},{2,1},{3,2},{4,7},{5,4},{6,5},{7,6},{8,11},{9,8},{10,9... | collective-permute-start | bytes 1806344 | tf_op jit(solution)/shard_map/ppermute | solution.py:21
  61.0 27.8 %collective-permute-start.15 = (f32[392,384]{1,0:T(8,128)S(1)}, f32[392,384]{1,0:T(8,128)S(1)}, u32[]{:S(2)}, u32[]{:S(2)}) collective-permute-start(f32[392,384]{1,0:T(8,128)S(1)} %pick_own.1), channel_id=1, source_target_pairs={{0,1},{1,2},{2,3},{3,0},{4,5},{5,6},{6,7},{7,4},{8,9},{9,10},{10,1... | collective-permute-start | bytes 1806344 | tf_op jit(solution)/shard_map/ppermute | solution.py:21
  64.6 41.4 %collective-permute-start.18 = (f32[384,384]{1,0:T(8,128)S(1)}, f32[384,384]{1,0:T(8,128)S(1)}, u32[]{:S(2)}, u32[]{:S(2)}) collective-permute-start(f32[384,384]{1,0:T(8,128)S(1)} %get-tuple-element.32.square_ref), channel_id=1, source_target_pairs={{0,24},{8,0},{16,8},{24,16},{1,25},{9,1},{17,9},{25,17},{2,26},{10... | collective-permute-start | bytes 1769480 | tf_op jit(solution)/shard_map/ppermute | solution.py:21
  65.8 40.2 %collective-permute-start.19 = (f32[384,384]{1,0:T(8,128)S(1)}, f32[384,384]{1,0:T(8,128)S(1)}, u32[]{:S(2)}, u32[]{:S(2)}) collective-permute-start(f32[384,384]{1,0:T(8,128)S(1)} %get-tuple-element.32.square_ref), channel_id=1, source_target_pairs={{0,8},{8,16},{16,24},{24,0},{1,9},{9,17},{17,25},{25,1},{2,10},{10... | collective-permute-start | bytes 1769480 | tf_op jit(solution)/shard_map/ppermute | solution.py:21
  65.8 45.9 %collective-permute-start.16 = (f32[384,384]{1,0:T(8,128)S(1)}, f32[384,384]{1,0:T(8,128)S(1)}, u32[]{:S(2)}, u32[]{:S(2)}) collective-permute-start(f32[384,384]{1,0:T(8,128)S(1)} %get-tuple-element.32.square_ref), channel_id=1, source_target_pairs={{0,4},{4,0},{1,5},{5,1},{2,6},{6,2},{3,7},{7,3},{8,12},{12,8},{9,1... | collective-permute-start | bytes 1769480 | tf_op jit(solution)/shard_map/ppermute | solution.py:21
  75.0 42.2 %collective-permute-start.12 = (f32[384,384]{1,0:T(8,128)S(1)}, f32[384,384]{1,0:T(8,128)S(1)}, u32[]{:S(2)}, u32[]{:S(2)}) collective-permute-start(f32[384,384]{1,0:T(8,128)S(1)} %get-tuple-element.32.square_ref), channel_id=1, source_target_pairs={{0,3},{1,0},{2,1},{3,2},{4,7},{5,4},{6,5},{7,6},{8,11},{9,8},{10,9... | collective-permute-start | bytes 1769480 | tf_op jit(solution)/shard_map/ppermute | solution.py:21
  88.8 28.4 %collective-permute-start.13 = (f32[384,384]{1,0:T(8,128)S(1)}, f32[384,384]{1,0:T(8,128)S(1)}, u32[]{:S(2)}, u32[]{:S(2)}) collective-permute-start(f32[384,384]{1,0:T(8,128)S(1)} %get-tuple-element.32.square_ref), channel_id=1, source_target_pairs={{0,1},{1,2},{2,3},{3,0},{4,5},{5,6},{6,7},{7,4},{8,9},{9,10},{10,1... | collective-permute-start | bytes 1769480 | tf_op jit(solution)/shard_map/ppermute | solution.py:21
  (1 other events, 2.2 us)

commit v2 on v1

v2 whole, which is shorter than its diff:
```python
import jax
import jax.numpy as jnp
from jax import lax
from jax.experimental import pallas as pl
from jax.experimental.pallas import tpu as pltpu
from jax.sharding import PartitionSpec as P

TARGET_RMS = 1.0
SIDES = (("gz", 5), ("gy", 3), ("gx", 1))
LOCAL_ORDER = (("gx", 1), ("gy", 3), ("gz", 5))
SWAP_AXIS = "gz"
SCALE = 2.0**30
ROWS = 8
LANES = 128
WORD = jnp.float32
HALF = jnp.bfloat16
VMEM_BYTES = 16 * 2**20

HBM = pl.BlockSpec(memory_space=pltpu.HBM)
VMEM = pl.BlockSpec(memory_space=pltpu.VMEM)
SMEM = pl.BlockSpec(memory_space=pltpu.SMEM)
PARAMS = pltpu.CompilerParams(vmem_limit_bytes=VMEM_BYTES)


def swaps(axis):
    count = lax.axis_size(axis)
    return axis == SWAP_AXIS and count > 2 and count % 2 == 0


def way(axis, r):
    if swaps(axis):
        return (lax.axis_index(axis) + r) % 2
    return r


def passed_along(value, axis, steps):
    count = lax.axis_size(axis)
    pairs = [(source, (source + steps) % count) for source in range(count)]
    return lax.ppermute(value, axis, pairs)


def exchanged(outgoing, axis):
    count = lax.axis_size(axis)
    if swaps(axis):
        results = []
        for r in range(2):
            pairs = [(i, (i + 1 if (i + r) % 2 == 0 else i - 1) % count) for i in range(count)]
            results.append(lax.ppermute(outgoing[r], axis, pairs))
        return results
    return [passed_along(outgoing[1], axis, -1), passed_along(outgoing[0], axis, 1)]


def partners_along(picked, axis):
    if lax.axis_size(axis) == 2:
        joined = passed_along(picked[0][0], axis, 1)
        return [(joined, 1), (joined, 0)]
    return [(got, None) for got in exchanged([a for a, _ in picked], axis)]


def faces_along(block, axis):
    if lax.axis_size(axis) == 2:
        return [passed_along(block, axis, 1)] * 2
    return exchanged([block, block], axis)


def all_along(value, axis):
    steps = range(1, lax.axis_size(axis))
    return [value] + [passed_along(value, axis, k) for k in steps]


def struct(*shape, dtype=WORD):
    return jax.ShapeDtypeStruct(shape, dtype)


def split(value):
    high = value.astype(HALF)
    return high, (value - high.astype(WORD)).astype(HALF)


def dot(left, right):
    return jnp.dot(left, right, preferred_element_type=WORD)


def beside(*values):
    return jnp.concatenate(values, axis=1)


def below(*values):
    return jnp.concatenate(values, axis=0)


def dot3(left, right):
    width = right[0].shape[1]
    wide = dot(left[0], beside(*right))
    return (wide[:, width:] + dot(left[1], right[0])) + wide[:, :width]


def dot3_sum(lefts, rights):
    left = [beside(*(pair[part] for pair in lefts)) for part in (0, 1)]
    right = [below(*(pair[part] for pair in rights)) for part in (0, 1)]
    return dot3(left, right)


def dot3_wide(left, rights):
    high, low = (beside(*(pair[part] for pair in rights)) for part in (0, 1))
    wide = dot(beside(*left), below(high, high)) + dot(left[0], low)
    width = wide.shape[1] // len(rights)
    return [wide[:, i * width : (i + 1) * width] for i in range(len(rights))]


def both(pair, s):
    return pair[0][s], pair[1][s]


def read(ref, place):
    return ref[...] if place is None else ref[place]


def tiled(row, width):
    return beside(*[row] * (width // LANES))


def pick_pair(raw, axis, slot):
    width = raw.shape[-1]
    joined = lax.axis_size(axis) == 2
    block = struct(width, width)
    shapes = [struct(2, width, width)] if joined else [block, block]

    def kernel(raw_ref, *rest):
        *outs, sem = rest
        copies = []
        for r, out in enumerate(outs):
            source = raw_ref.at[pl.ds(slot, 2) if joined else slot + way(axis, r)]
            copies.append(pltpu.make_async_copy(source, out, sem.at[r]))
        for copy in copies:
            copy.start()
        for copy in copies:
            copy.wait()

    picked = pl.pallas_call(
        kernel,
        in_specs=[HBM],
        out_specs=[VMEM] * len(shapes),
        out_shape=shapes,
        scratch_shapes=[pltpu.SemaphoreType.DMA((len(shapes),))],
        compiler_params=PARAMS,
    )(raw)
    if joined:
        return [(picked[0], 0), (picked[0], 1)]
    return [(block, None) for block in picked]


def pick_own(raw, keep):
    slots, width = raw.shape[0], raw.shape[-1]

    def kernel(raw_ref, keep_ref, own, rows, own_and_rows, sem):
        targets = (own, own_and_rows.at[pl.ds(0, width)])
        copies = [
            pltpu.make_async_copy(raw_ref.at[0], target, sem.at[i])
            for i, target in enumerate(targets)
        ]
        for copy in copies:
            copy.start()
        row = lax.broadcasted_iota(jnp.int32, (ROWS, width), 0)
        tile = jnp.zeros((ROWS, width), WORD)
        for s in range(slots):
            tile = jnp.where(row == s, keep_ref[s].astype(WORD), tile)
        rows[...] = tile
        own_and_rows[pl.ds(width, ROWS), :] = tile
        for copy in copies:
            copy.wait()

    return pl.pallas_call(
        kernel,
        in_specs=[HBM, SMEM],
        out_specs=[VMEM] * 3,
        out_shape=[
            struct(width, width),
            struct(ROWS, width),
            struct(width + ROWS, width),
        ],
        scratch_shapes=[pltpu.SemaphoreType.DMA((2,))],
        compiler_params=PARAMS,
        name="pick_own",
    )(raw, keep)


def first_products(raw, keep_rows):
    slots, width = raw.shape[0], raw.shape[-1]

    def kernel(block_ref, keep_ref, high_ref, low_ref, product_ref, tile_ref, total):
        s = pl.program_id(0)
        block = block_ref[0]
        half = split(block * SCALE)
        high_ref[s], low_ref[s] = half

        @pl.when(s == 0)
        def _():
            total[...] = jnp.zeros_like(total)

        product_ref[s] = dot3((high_ref[0], low_ref[0]), half)
        total[...] += jnp.sum((block * block).reshape(-1, ROWS, width), axis=0)

        @pl.when(s == pl.num_programs(0) - 1)
        def _():
            row = lax.broadcasted_iota(jnp.int32, (ROWS, LANES), 0)
            norm = jnp.full((ROWS, LANES), jnp.sum(total[...]), WORD)
            tile_ref[...] = jnp.where(row == ROWS - 1, norm, keep_ref[:, :LANES])

    return pl.pallas_call(
        kernel,
        grid=(slots,),
        in_specs=[pl.BlockSpec((1, width, width), lambda s: (s, 0, 0)), VMEM],
        out_specs=[VMEM] * 4,
        out_shape=[
            struct(*raw.shape, dtype=HALF),
            struct(*raw.shape, dtype=HALF),
            struct(*raw.shape),
            struct(ROWS, LANES),
        ],
        scratch_shapes=[pltpu.VMEM((ROWS, width), WORD)],
        compiler_params=PARAMS,
        name="first_products",
    )(raw, keep_rows)


def side_products(halves, axis, slot, partners, products=None, others=()):
    width = halves[0].shape[-1]
    operands = [*halves, partners[0][0], partners[1][0]]
    out_shape = [struct(2, width, width)]
    if products is not None:
        operands += [products, *others]
        out_shape.append(struct(width, width))

    def kernel(high, low, first, second, *rest):
        values = []
        for r, (ref, (_, place)) in enumerate(zip((first, second), partners)):
            half = both((high, low), slot + way(axis, r))
            values.append(dot3(half, split(read(ref, place) * SCALE)))
        if products is None:
            (side_ref,) = rest
        else:
            own, *sides, side_ref, square_ref = rest
            total = own[0]
            for other in sides:
                total = total + (other[0] + other[1])
            square_ref[...] = total + (values[0] + values[1])
        side_ref[0] = values[0]
        side_ref[1] = values[1]

    return pl.pallas_call(
        kernel,
        in_specs=[VMEM] * len(operands),
        out_specs=[VMEM] * len(out_shape),
        out_shape=out_shape,
        compiler_params=PARAMS,
    )(*operands)


def cube_parts(keep_rows, halves, axis, slot, faces, nears, partners, products, side):
    width = halves[0].shape[-1]
    apart = nears is not None

    def kernel(keep, high, low, f0, f1, p0, p1, products, side, *rest):
        *tiles, pair, near, mix = rest
        squares, lefts, values, mixes = [], [], [], []
        for r, (face, ref, (_, place)) in enumerate(zip((f0, f1), (p0, p1), partners)):
            turn = way(axis, r)
            s = slot + turn
            back = slot + 1 - turn
            if not apart:
                near_keep = face[pl.ds(width + back, 1), :]
            elif isinstance(turn, int):
                near_keep = tiled(tiles[r][pl.ds(back, 1), :], width)
            else:
                here, there = (t[pl.ds(back, 1), :] for t in tiles)
                near_keep = tiled(jnp.where(turn == 0, here, there), width)
            coupled = dot3(both((high, low), s), split(face[:width] * SCALE))
            squares.append(split(keep[pl.ds(s, 1), :] * (products[s] + coupled)))
            lefts.append(split(near_keep * coupled))
            values.append(split(read(ref, place) * SCALE))
            mixes.append(near_keep * side[r])
        pair[0], pair[1] = dot3_wide(both((high, low), 0), squares)
        near[...] = dot3_sum(lefts, values)
        mix[...] = mixes[0] + mixes[1]

    operands = [keep_rows, *halves, *faces, partners[0][0], partners[1][0]]
    operands += [products, side, *(nears or ())]
    return pl.pallas_call(
        kernel,
        in_specs=[VMEM] * len(operands),
        out_specs=[VMEM] * 3,
        out_shape=[
            struct(2, width, width),
            struct(width, width),
            struct(width, width),
        ],
        compiler_params=PARAMS,
    )(*operands)


def own_cube(halves, square, parts):
    width = square.shape[-1]

    def kernel(high, low, square_ref, *rest):
        *refs, out = rest
        near, mix = refs[0][...], refs[1][...]
        for ref in refs[2::2]:
            near = near + ref[...]
        for ref in refs[3::2]:
            mix = mix + ref[...]
        own = both((high, low), 0)
        out[...] = near + dot3_sum((own, split(mix)), (split(square_ref[...]), own))

    return pl.pallas_call(
        kernel,
        in_specs=[VMEM] * (3 + len(parts)),
        out_specs=VMEM,
        out_shape=struct(width, width),
        compiler_params=PARAMS,
        name="own_cube",
    )(*halves, square, *parts)


def total_of(tiles):
    def kernel(*refs):
        *parts, out = refs
        total = parts[0][...]
        for part in parts[1:]:
            total = total + part[...]
        out[...] = total

    return pl.pallas_call(
        kernel,
        in_specs=[VMEM] * len(tiles),
        out_specs=VMEM,
        out_shape=struct(ROWS, LANES),
        compiler_params=PARAMS,
        name="total_of",
    )(*tiles)


def outputs_of(
    norms, entry_count, keep_rows, halves, axis, slot, raws, faces, part, own=None, out=None
):
    width = part.shape[-1]
    shape = halves[0].shape
    count = len(norms)
    chunk = width // 2

    def kernel(*refs):
        norm_refs, rest = refs[:count], refs[count:]
        keep, high, low, raw0, raw1, f0, f1, part_ref, *rest = rest
        *given, out_ref, staged, sem = rest
        norm_sq = norm_refs[0][ROWS - 1 :, :]
        for ref in norm_refs[1:]:
            norm_sq = norm_sq + ref[ROWS - 1 :, :]
        factor = tiled(TARGET_RMS / jnp.sqrt(norm_sq / entry_count), width)
        small = factor * (1.0 / SCALE)
        copies = []

        def put(place, s, rows, raw, cube):
            kept = keep[pl.ds(s, 1), :]
            staged[place, rows, :] = kept * (
                (1.5 * factor) * raw - 0.5 * (((cube * small) * small) * small)
            )
            copy = pltpu.make_async_copy(
                staged.at[place, rows],
                out_ref.at[s, rows],
                sem.at[len(copies)],
            )
            copy.start()
            copies.append(copy)

        if own is not None:
            own_ref, cube_ref = given
            put(2, 0, pl.ds(0, width), own_ref[...], cube_ref[...])
        for r, (raw_ref, face) in enumerate(((raw0, f0), (raw1, f1))):
            s = slot + way(axis, r)
            right = split(face[...])
            for start in range(0, width, chunk):
                rows = pl.ds(start, chunk)
                left = (high[s, rows, :], low[s, rows, :])
                cube = part_ref[r, rows, :] + dot3(left, right)
                place = raws[r][1]
                raw = raw_ref[rows, :] if place is None else raw_ref[place, rows, :]
                put(r, s, rows, raw, cube)
        for copy in copies:
            copy.wait()

    operands = [*norms, keep_rows, *halves, raws[0][0], raws[1][0], *faces, part]
    operands += own if own is not None else []
    in_specs = [VMEM] * len(operands)
    aliases = {}
    if out is not None:
        aliases = {len(operands): 0}
        operands.append(out)
        in_specs.append(HBM)
    return pl.pallas_call(
        kernel,
        in_specs=in_specs,
        out_specs=HBM,
        out_shape=struct(*shape),
        scratch_shapes=[
            pltpu.VMEM((3, width, width), WORD),
            pltpu.SemaphoreType.DMA((5,)),
        ],
        input_output_aliases=aliases,
        compiler_params=PARAMS,
    )(*operands)


def body(hamiltonian, keep_mask):
    return step(hamiltonian[0, 0, 0], keep_mask[0, 0, 0])[None, None, None]


def step(raw, keep):
    raw = pltpu.with_memory_space_constraint(raw, pltpu.HBM)
    entry_count = raw.shape[-1]
    for axis, _ in SIDES:
        entry_count = entry_count * lax.axis_size(axis)

    picked, partners, faces, nears, square_faces, side, parts = ({} for _ in range(7))
    for axis, slot in SIDES:
        picked[slot] = pick_pair(raw, axis, slot)
        partners[slot] = partners_along(picked[slot], axis)
    own, keep_rows, own_and_rows = pick_own(raw, keep)
    high, low, products, tile = first_products(raw, keep_rows)
    halves = (high, low)

    norms = [tile]
    for axis, slot in SIDES:
        if len(norms) > 1:
            norms = [total_of(norms)]
        norms = all_along(norms[0], axis)
        if axis == SWAP_AXIS:
            nears[slot] = [norms[-1], norms[1]]
    for axis, slot in SIDES:
        payload = own_and_rows if slot not in nears else own
        faces[slot] = faces_along(payload, axis)

    for axis, slot in LOCAL_ORDER[:-1]:
        (side[slot],) = side_products(halves, axis, slot, partners[slot])
    axis, slot = LOCAL_ORDER[-1]
    side[slot], square = side_products(
        halves, axis, slot, partners[slot], products, tuple(side.values())
    )
    for axis, slot in SIDES:
        square_faces[slot] = faces_along(square, axis)

    sums = []
    for axis, slot in LOCAL_ORDER:
        parts[slot], near, mix = cube_parts(
            keep_rows,
            halves,
            axis,
            slot,
            faces[slot],
            nears.get(slot),
            partners[slot],
            products,
            side[slot],
        )
        sums += [near, mix]
    cube = own_cube(halves, square, sums)

    out = None
    for axis, slot in LOCAL_ORDER:
        out = outputs_of(
            norms,
            entry_count,
            keep_rows,
            halves,
            axis,
            slot,
            picked[slot],
            square_faces[slot],
            parts[slot],
            own=[own, cube] if out is None else None,
            out=out,
        )
    return out


def solution(mesh):
    placed = (P("gx", "gy", "gz", None, None, None), P("gx", "gy", "gz", None))
    return jax.shard_map(
        body,
        mesh=mesh,
        in_specs=placed,
        out_specs=P("gx", "gy", "gz", None, None, None),
        check_vma=False,
    )
```

time: 123 us -> 141 us (1.15)
  waiting for transfers between devices: 42.6 us -> 67.7 us
  Pallas kernels: 48.5 us -> 33.5 us
  starting transfers between devices: 29.2 us -> 38.9 us
  local copies, waits for them, and re-layouts: 2.18 us -> 0.01 us
    ppermute x0 -> x6, waiting for transfers between devices: none -> 45.5 us  [exchanged(): results.append(lax.ppermute(outgoing[r], axis, pairs))]
    ppermute x0 -> x6, starting transfers between devices: none -> 21.7 us  [exchanged(): results.append(lax.ppermute(outgoing[r], axis, pairs))]
    ppermute x22 -> x16, waiting for transfers between devices: 42.6 us -> 22.2 us  [passed_along(): return lax.ppermute(value, axis, pairs)]
    pallas_call x11 -> x10, Pallas kernels: 43.1 us -> 24.9 us  [the longest x3 8.97 us: cube_parts(): pl.pallas_call(kernel, in_specs=[VMEM] * len(operands), out_specs=[VMEM]...]
    ppermute x22 -> x16, starting transfers between devices: 29.2 us -> 17.2 us  [passed_along(): return lax.ppermute(value, axis, pairs)]
    pallas_call x3, Pallas kernels: 0.76 us -> 3.81 us  [pick_pair(): pl.pallas_call(kernel, in_specs=[HBM], out_specs=[VMEM] * len(shapes), ou...]
    unnamed x6 -> x2, local copies, waits for them, and re-layouts: 2.18 us -> 0.01 us
  transfers between devices with their start and end apart: 22 -> 22, of which waited for: 7 -> 9; matrix products, arithmetic and copies ran while one was open for 0% -> 0% of each run, Pallas kernels for 35% -> 21%
where the time goes in v2:
time: 141 us; the launch traced here: 140 us
  waiting for transfers between devices  67.7 us (48%)
  starting transfers between devices  38.9 us (28%)
  Pallas kernels  33.5 us (24%)
    ppermute x6, waiting for transfers between devices, exchanged(): results.append(lax.ppermute(outgoing[r], axis, pairs))  45.5 us
    ppermute x16, waiting for transfers between devices, passed_along(): return lax.ppermute(value, axis, pairs)  22.2 us
    ppermute x6, starting transfers between devices, exchanged(): results.append(lax.ppermute(outgoing[r], axis, pairs))  21.7 us
    ppermute x16, starting transfers between devices, passed_along(): return lax.ppermute(value, axis, pairs)  17.2 us
    pallas_call x3, Pallas kernels, cube_parts(): pl.pallas_call(kernel, in_specs=[VMEM] * len(operands), out_specs=[VMEM]...  8.97 us
    pallas_call x1, Pallas kernels, first_products(): pl.pallas_call(kernel, grid=(slots,), in_specs=[pl.BlockSpec((1, width, w...  7.66 us
    pallas_call x3, Pallas kernels, outputs_of(): pl.pallas_call(kernel, in_specs=in_specs, out_specs=HBM, out_shape=struct...  6.47 us
    pallas_call x3, Pallas kernels, pick_pair(): pl.pallas_call(kernel, in_specs=[HBM], out_specs=[VMEM] * len(shapes), ou...  3.81 us
  transfers between devices with their start and end apart: 22, of which 9 were waited for; matrix products, arithmetic and copies ran while one was open for 0% of the time, Pallas kernels for 21%

profile of v2, /device:TPU:0, one launch (start us, length us, event | category | flops | bytes accessed | tf_op | source)
XLA Modules:
  0.0 140.4 jit_solution(8358985835791619426)
XLA Ops:
  1.3 3.1 %collective-permute-start.11 = (f32[2,384,384]{2,1,0:T(8,128)S(1)}, f32[2,384,384]{2,1,0:T(8,128)S(1)}, u32[]{:S(2)}, u32[]{:S(2)}) collective-permute-start(f32[2,384,384]{2,1,0:T(8,128)S(1)} %shard_map.31.refs_7_.refs_8_), channel_id=1, source_target_pairs={{0,4},{4,0},{1,5},{5,1},{2,6},{6,2},{3,7},{7,3},{8,12},{12,8},{9,1... | collective-permute-start | bytes 3538952 | tf_op jit(solution)/shard_map/ppermute | solution.py:39
  4.4 1.8 %pick_own.1 = (f32[384,384]{1,0:T(8,128)S(1)}, f32[8,384]{1,0:T(8,128)S(1)}, f32[392,384]{1,0:T(8,128)S(1)}) custom-call(f32[7,384,384]{2,1,0:T(8,128)} %bitcast.5, s32[7]{0:T(128)S(1)} %bitcast.3), custom_call_target="tpu_custom_call" | custom-call | tf_op jit(solution)/shard_map/pick_own/pallas_call | solution.py:173
  6.2 7.7 %first_products.1 = (bf16[7,384,384]{2,1,0:T(8,128)(2,1)S(1)}, bf16[7,384,384]{2,1,0:T(8,128)(2,1)S(1)}, f32[7,384,384]{2,1,0:T(8,128)S(1)}, f32[8,128]{1,0:T(8,128)S(1)}) custom-call(f32[7,384,384]{2,1,0:T(8,128)} %bitcast.6, f32[8,384]{1,0:T(8,128)S(1)} %get-tuple-element.27.keep_ref.keep.refs_4_), custom_call_target="tpu_custom_call" | custom-call | tf_op jit(solution)/shard_map/first_products/pallas_call | solution.py:210
  13.8 1.6 %collective-permute-start = (f32[8,128]{1,0:T(8,128)S(1)}, f32[8,128]{1,0:T(8,128)S(1)}, u32[]{:S(2)}, u32[]{:S(2)}) collective-permute-start(f32[8,128]{1,0:T(8,128)S(1)} %get-tuple-element.28.refs_0_), channel_id=1, source_target_pairs={{0,1},{1,2},{2,3},{3,0},{4,5},{5,6},{6,7},{7,4},{8,9},{9,10},{10,1... | collective-permute-start | bytes 12296 | tf_op jit(solution)/shard_map/ppermute | solution.py:39
  15.5 2.2 %collective-permute-start.2 = (f32[8,128]{1,0:T(8,128)S(1)}, f32[8,128]{1,0:T(8,128)S(1)}, u32[]{:S(2)}, u32[]{:S(2)}) collective-permute-start(f32[8,128]{1,0:T(8,128)S(1)} %get-tuple-element.28.refs_0_), channel_id=1, source_target_pairs={{0,3},{1,0},{2,1},{3,2},{4,7},{5,4},{6,5},{7,6},{8,11},{9,8},{10,9... | collective-permute-start | bytes 12296 | tf_op jit(solution)/shard_map/ppermute | solution.py:39
  19.3 2.9 %collective-permute-done.1.refs_2_ = f32[8,128]{1,0:T(8,128)S(1)} collective-permute-done((f32[8,128]{1,0:T(8,128)S(1)}, f32[8,128]{1,0:T(8,128)S(1)}, u32[]{:S(2)}, u32[]{:S(2)}) %collective-permute-start.1) | collective-permute-done | bytes 4128 | tf_op jit(solution)/shard_map/ppermute | solution.py:39
  22.6 7.8 %collective-permute-done.3.refs_1_ = f32[8,128]{1,0:T(8,128)S(1)} collective-permute-done((f32[8,128]{1,0:T(8,128)S(1)}, f32[8,128]{1,0:T(8,128)S(1)}, u32[]{:S(2)}, u32[]{:S(2)}) %collective-permute-start.3) | collective-permute-done | bytes 4128 | tf_op jit(solution)/shard_map/ppermute | solution.py:39
  31.7 1.9 %collective-permute-start.10 = (f32[384,384]{1,0:T(8,128)S(1)}, f32[384,384]{1,0:T(8,128)S(1)}, u32[]{:S(2)}, u32[]{:S(2)}) collective-permute-start(f32[384,384]{1,0:T(8,128)S(1)} %get-tuple-element.35.refs_7_), channel_id=1, source_target_pairs={{0,8},{8,16},{16,24},{24,0},{1,9},{9,17},{17,25},{25,1},{2,10},{10... | collective-permute-start | bytes 1769480 | tf_op jit(solution)/shard_map/ppermute | solution.py:39
  34.8 1.8 %collective-permute-start.7 = (f32[384,384]{1,0:T(8,128)S(1)}, f32[384,384]{1,0:T(8,128)S(1)}, u32[]{:S(2)}, u32[]{:S(2)}) collective-permute-start(f32[384,384]{1,0:T(8,128)S(1)} %get-tuple-element.31.refs_7_), channel_id=1, source_target_pairs={{0,1},{1,0},{2,3},{3,2},{4,5},{5,4},{6,7},{7,6},{8,9},{9,8},{10,11... | collective-permute-start | bytes 1769480 | tf_op jit(solution)/shard_map/ppermute | solution.py:48
  38.2 9.3 %collective-permute-done.5.refs_2_ = f32[8,128]{1,0:T(8,128)S(1)} collective-permute-done((f32[8,128]{1,0:T(8,128)S(1)}, f32[8,128]{1,0:T(8,128)S(1)}, u32[]{:S(2)}, u32[]{:S(2)}) %collective-permute-start.5) | collective-permute-done | bytes 4128 | tf_op jit(solution)/shard_map/ppermute | solution.py:39
  49.5 3.4 %collective-permute-start.8 = (f32[384,384]{1,0:T(8,128)S(1)}, f32[384,384]{1,0:T(8,128)S(1)}, u32[]{:S(2)}, u32[]{:S(2)}) collective-permute-start(f32[384,384]{1,0:T(8,128)S(1)} %get-tuple-element.32.refs_8_), channel_id=1, source_target_pairs={{0,3},{1,2},{2,1},{3,0},{4,7},{5,6},{6,5},{7,4},{8,11},{9,10},{10,... | collective-permute-start | bytes 1769480 | tf_op jit(solution)/shard_map/ppermute | solution.py:48
  56.0 11.4 %collective-permute-done.8.second.p1 = f32[384,384]{1,0:T(8,128)S(1)} collective-permute-done((f32[384,384]{1,0:T(8,128)S(1)}, f32[384,384]{1,0:T(8,128)S(1)}, u32[]{:S(2)}, u32[]{:S(2)}) %collective-permute-start.8) | collective-permute-done | bytes 589856 | tf_op jit(solution)/shard_map/ppermute | solution.py:48
  67.3 12.0 %collective-permute-start.14 = (f32[384,384]{1,0:T(8,128)S(1)}, f32[384,384]{1,0:T(8,128)S(1)}, u32[]{:S(2)}, u32[]{:S(2)}) collective-permute-start(f32[384,384]{1,0:T(8,128)S(1)} %get-tuple-element.37.refs_12_), channel_id=1, source_target_pairs={{0,1},{1,0},{2,3},{3,2},{4,5},{5,4},{6,7},{7,6},{8,9},{9,8},{10,11... | collective-permute-start | bytes 1769480 | tf_op jit(solution)/shard_map/ppermute | solution.py:48
  79.3 2.5 %collective-permute-start.15 = (f32[384,384]{1,0:T(8,128)S(1)}, f32[384,384]{1,0:T(8,128)S(1)}, u32[]{:S(2)}, u32[]{:S(2)}) collective-permute-start(f32[384,384]{1,0:T(8,128)S(1)} %get-tuple-element.37.refs_12_), channel_id=1, source_target_pairs={{0,3},{1,2},{2,1},{3,0},{4,7},{5,6},{6,5},{7,4},{8,11},{9,10},{10,... | collective-permute-start | bytes 1769480 | tf_op jit(solution)/shard_map/ppermute | solution.py:48
  85.5 7.6 %collective-permute-done.14.f0 = f32[384,384]{1,0:T(8,128)S(1)} collective-permute-done((f32[384,384]{1,0:T(8,128)S(1)}, f32[384,384]{1,0:T(8,128)S(1)}, u32[]{:S(2)}, u32[]{:S(2)}) %collective-permute-start.14) | collective-permute-done | bytes 589856 | tf_op jit(solution)/shard_map/ppermute | solution.py:48
  93.5 14.3 %collective-permute-done.15.f1 = f32[384,384]{1,0:T(8,128)S(1)} collective-permute-done((f32[384,384]{1,0:T(8,128)S(1)}, f32[384,384]{1,0:T(8,128)S(1)}, u32[]{:S(2)}, u32[]{:S(2)}) %collective-permute-start.15) | collective-permute-done | bytes 589856 | tf_op jit(solution)/shard_map/ppermute | solution.py:48
  109.4 2.0 %collective-permute-start.13 = (f32[384,384]{1,0:T(8,128)S(1)}, f32[384,384]{1,0:T(8,128)S(1)}, u32[]{:S(2)}, u32[]{:S(2)}) collective-permute-start(f32[384,384]{1,0:T(8,128)S(1)} %get-tuple-element.36.square_ref), channel_id=1, source_target_pairs={{0,3},{1,2},{2,1},{3,0},{4,7},{5,6},{6,5},{7,4},{8,11},{9,10},{10,... | collective-permute-start | bytes 1769480 | tf_op jit(solution)/shard_map/ppermute | solution.py:48
  111.5 3.0 %shard_map.36 = (f32[2,384,384]{2,1,0:T(8,128)S(1)}, f32[384,384]{1,0:T(8,128)S(1)}, f32[384,384]{1,0:T(8,128)S(1)}) custom-call(f32[8,384]{1,0:T(8,128)S(1)} %get-tuple-element.27.keep_ref.keep.refs_4_, bf16[7,384,384]{2,1,0:T(8,128)(2,1)S(1)} %get-tuple-element.29.high.refs_5_, bf16[7,384,384]{2,1,0:T(8,128)(2,1)S(1)} %get-tuple-element.30.low.refs_6_, ...), custom_call_target="tpu_custom_call" | custom-call | tf_op jit(solution)/shard_map/pallas_call | solution.py:289
  114.4 3.0 %shard_map.35 = (f32[2,384,384]{2,1,0:T(8,128)S(1)}, f32[384,384]{1,0:T(8,128)S(1)}, f32[384,384]{1,0:T(8,128)S(1)}) custom-call(f32[8,384]{1,0:T(8,128)S(1)} %get-tuple-element.27.keep_ref.keep.refs_4_, bf16[7,384,384]{2,1,0:T(8,128)(2,1)S(1)} %get-tuple-element.29.high.refs_5_, bf16[7,384,384]{2,1,0:T(8,128)(2,1)S(1)} %get-tuple-element.30.low.refs_6_, ...), custom_call_target="tpu_custom_call" | custom-call | tf_op jit(solution)/shard_map/pallas_call | solution.py:289
  117.4 3.0 %shard_map.34 = (f32[2,384,384]{2,1,0:T(8,128)S(1)}, f32[384,384]{1,0:T(8,128)S(1)}, f32[384,384]{1,0:T(8,128)S(1)}) custom-call(f32[8,384]{1,0:T(8,128)S(1)} %get-tuple-element.27.keep_ref.keep.refs_4_, bf16[7,384,384]{2,1,0:T(8,128)(2,1)S(1)} %get-tuple-element.29.high.refs_5_, bf16[7,384,384]{2,1,0:T(8,128)(2,1)S(1)} %get-tuple-element.30.low.refs_6_, ...), custom_call_target="tpu_custom_call" | custom-call | tf_op jit(solution)/shard_map/pallas_call | solution.py:289
  121.5 2.3 %shard_map.37.refs_12_ = f32[7,384,384]{2,1,0:T(8,128)} custom-call(f32[8,128]{1,0:T(8,128)S(1)} %total_of.3.refs_0_, f32[8,128]{1,0:T(8,128)S(1)} %collective-permute-done.4.refs_1_, f32[8,128]{1,0:T(8,128)S(1)} %collective-permute-done.5.refs_2_, f32[8,128]{1,0:T(8,128)S(1)} %collective-permute-done.6.refs_3_, ...), custom_call_target="tpu_custom_call" | custom-call | tf_op jit(solution)/shard_map/pallas_call | solution.py:399
  123.8 2.1 %shard_map.38.refs_12_ = f32[7,384,384]{2,1,0:T(8,128)} custom-call(f32[8,128]{1,0:T(8,128)S(1)} %total_of.3.refs_0_, f32[8,128]{1,0:T(8,128)S(1)} %collective-permute-done.4.refs_1_, f32[8,128]{1,0:T(8,128)S(1)} %collective-permute-done.5.refs_2_, f32[8,128]{1,0:T(8,128)S(1)} %collective-permute-done.6.refs_3_, ...), custom_call_target="tpu_custom_call", output_to_operand_aliasing={{}: (12, {})} | custom-call | tf_op jit(solution)/shard_map/pallas_call | solution.py:399
  126.0 12.2 %collective-permute-done.13.refs_10_ = f32[384,384]{1,0:T(8,128)S(1)} collective-permute-done((f32[384,384]{1,0:T(8,128)S(1)}, f32[384,384]{1,0:T(8,128)S(1)}, u32[]{:S(2)}, u32[]{:S(2)}) %collective-permute-start.13) | collective-permute-done | bytes 589856 | tf_op jit(solution)/shard_map/ppermute | solution.py:48
  138.1 2.1 %shard_map.39 = f32[7,384,384]{2,1,0:T(8,128)} custom-call(f32[8,128]{1,0:T(8,128)S(1)} %total_of.3.refs_0_, f32[8,128]{1,0:T(8,128)S(1)} %collective-permute-done.4.refs_1_, f32[8,128]{1,0:T(8,128)S(1)} %collective-permute-done.5.refs_2_, f32[8,128]{1,0:T(8,128)S(1)} %collective-permute-done.6.refs_3_, ...), custom_call_target="tpu_custom_call", output_to_operand_aliasing={{}: (12, {})} | custom-call | tf_op jit(solution)/shard_map/pallas_call | solution.py:399
  (39 shorter events, 19.1 us)
Async XLA Ops:
  0.0 4.4 %copy-start = (s32[1,1,1,7]{3,2,1,0:T(1,128)S(1)}, s32[1,1,1,7]{3,2,1,0:T(1,128)}, u32[]{:S(2)}) copy-start(s32[1,1,1,7]{3,2,1,0:T(1,128)} %param.3) | copy-start | bytes 88
  1.3 78.0 %collective-permute-start.11 = (f32[2,384,384]{2,1,0:T(8,128)S(1)}, f32[2,384,384]{2,1,0:T(8,128)S(1)}, u32[]{:S(2)}, u32[]{:S(2)}) collective-permute-start(f32[2,384,384]{2,1,0:T(8,128)S(1)} %shard_map.31.refs_7_.refs_8_), channel_id=1, source_target_pairs={{0,4},{4,0},{1,5},{5,1},{2,6},{6,2},{3,7},{7,3},{8,12},{12,8},{9,1... | collective-permute-start | bytes 3538952 | tf_op jit(solution)/shard_map/ppermute | solution.py:39
  13.8 5.5 %collective-permute-start = (f32[8,128]{1,0:T(8,128)S(1)}, f32[8,128]{1,0:T(8,128)S(1)}, u32[]{:S(2)}, u32[]{:S(2)}) collective-permute-start(f32[8,128]{1,0:T(8,128)S(1)} %get-tuple-element.28.refs_0_), channel_id=1, source_target_pairs={{0,1},{1,2},{2,3},{3,0},{4,5},{5,6},{6,7},{7,4},{8,9},{9,10},{10,1... | collective-permute-start | bytes 12296 | tf_op jit(solution)/shard_map/ppermute | solution.py:39
  15.5 3.8 %collective-permute-start.2 = (f32[8,128]{1,0:T(8,128)S(1)}, f32[8,128]{1,0:T(8,128)S(1)}, u32[]{:S(2)}, u32[]{:S(2)}) collective-permute-start(f32[8,128]{1,0:T(8,128)S(1)} %get-tuple-element.28.refs_0_), channel_id=1, source_target_pairs={{0,3},{1,0},{2,1},{3,2},{4,7},{5,4},{6,5},{7,6},{8,11},{9,8},{10,9... | collective-permute-start | bytes 12296 | tf_op jit(solution)/shard_map/ppermute | solution.py:39
  17.7 4.5 %collective-permute-start.1 = (f32[8,128]{1,0:T(8,128)S(1)}, f32[8,128]{1,0:T(8,128)S(1)}, u32[]{:S(2)}, u32[]{:S(2)}) collective-permute-start(f32[8,128]{1,0:T(8,128)S(1)} %get-tuple-element.28.refs_0_), channel_id=1, source_target_pairs={{0,2},{1,3},{2,0},{3,1},{4,6},{5,7},{6,4},{7,5},{8,10},{9,11},{10,... | collective-permute-start | bytes 12296 | tf_op jit(solution)/shard_map/ppermute | solution.py:39
  22.2 8.2 %collective-permute-start.3 = (f32[8,128]{1,0:T(8,128)S(1)}, f32[8,128]{1,0:T(8,128)S(1)}, u32[]{:S(2)}, u32[]{:S(2)}) collective-permute-start(f32[8,128]{1,0:T(8,128)S(1)} %total_of.2.refs_0_), channel_id=1, source_target_pairs={{0,4},{4,0},{1,5},{5,1},{2,6},{6,2},{3,7},{7,3},{8,12},{12,8},{9,1... | collective-permute-start | bytes 12296 | tf_op jit(solution)/shard_map/ppermute | solution.py:39
  30.4 6.3 %collective-permute-start.4 = (f32[8,128]{1,0:T(8,128)S(1)}, f32[8,128]{1,0:T(8,128)S(1)}, u32[]{:S(2)}, u32[]{:S(2)}) collective-permute-start(f32[8,128]{1,0:T(8,128)S(1)} %total_of.3.refs_0_), channel_id=1, source_target_pairs={{0,8},{8,16},{16,24},{24,0},{1,9},{9,17},{17,25},{25,1},{2,10},{10... | collective-permute-start | bytes 12296 | tf_op jit(solution)/shard_map/ppermute | solution.py:39
  31.7 21.2 %collective-permute-start.10 = (f32[384,384]{1,0:T(8,128)S(1)}, f32[384,384]{1,0:T(8,128)S(1)}, u32[]{:S(2)}, u32[]{:S(2)}) collective-permute-start(f32[384,384]{1,0:T(8,128)S(1)} %get-tuple-element.35.refs_7_), channel_id=1, source_target_pairs={{0,8},{8,16},{16,24},{24,0},{1,9},{9,17},{17,25},{25,1},{2,10},{10... | collective-permute-start | bytes 1769480 | tf_op jit(solution)/shard_map/ppermute | solution.py:39
  33.6 20.8 %collective-permute-start.9 = (f32[384,384]{1,0:T(8,128)S(1)}, f32[384,384]{1,0:T(8,128)S(1)}, u32[]{:S(2)}, u32[]{:S(2)}) collective-permute-start(f32[384,384]{1,0:T(8,128)S(1)} %get-tuple-element.34.refs_8_), channel_id=1, source_target_pairs={{0,24},{8,0},{16,8},{24,16},{1,25},{9,1},{17,9},{25,17},{2,26},{10... | collective-permute-start | bytes 1769480 | tf_op jit(solution)/shard_map/ppermute | solution.py:39
  34.8 19.5 %collective-permute-start.7 = (f32[384,384]{1,0:T(8,128)S(1)}, f32[384,384]{1,0:T(8,128)S(1)}, u32[]{:S(2)}, u32[]{:S(2)}) collective-permute-start(f32[384,384]{1,0:T(8,128)S(1)} %get-tuple-element.31.refs_7_), channel_id=1, source_target_pairs={{0,1},{1,0},{2,3},{3,2},{4,5},{5,4},{6,7},{7,6},{8,9},{9,8},{10,11... | collective-permute-start | bytes 1769480 | tf_op jit(solution)/shard_map/ppermute | solution.py:48
  36.7 10.8 %collective-permute-start.5 = (f32[8,128]{1,0:T(8,128)S(1)}, f32[8,128]{1,0:T(8,128)S(1)}, u32[]{:S(2)}, u32[]{:S(2)}) collective-permute-start(f32[8,128]{1,0:T(8,128)S(1)} %total_of.3.refs_0_), channel_id=1, source_target_pairs={{0,16},{8,24},{16,0},{24,8},{1,17},{9,25},{17,1},{25,9},{2,18},{10... | collective-permute-start | bytes 12296 | tf_op jit(solution)/shard_map/ppermute | solution.py:39
  47.5 2.1 %collective-permute-start.6 = (f32[8,128]{1,0:T(8,128)S(1)}, f32[8,128]{1,0:T(8,128)S(1)}, u32[]{:S(2)}, u32[]{:S(2)}) collective-permute-start(f32[8,128]{1,0:T(8,128)S(1)} %total_of.3.refs_0_), channel_id=1, source_target_pairs={{0,24},{8,0},{16,8},{24,16},{1,25},{9,1},{17,9},{25,17},{2,26},{10... | collective-permute-start | bytes 12296 | tf_op jit(solution)/shard_map/ppermute | solution.py:39
  49.5 17.8 %collective-permute-start.8 = (f32[384,384]{1,0:T(8,128)S(1)}, f32[384,384]{1,0:T(8,128)S(1)}, u32[]{:S(2)}, u32[]{:S(2)}) collective-permute-start(f32[384,384]{1,0:T(8,128)S(1)} %get-tuple-element.32.refs_8_), channel_id=1, source_target_pairs={{0,3},{1,2},{2,1},{3,0},{4,7},{5,6},{6,5},{7,4},{8,11},{9,10},{10,... | collective-permute-start | bytes 1769480 | tf_op jit(solution)/shard_map/ppermute | solution.py:48
  52.9 55.0 %collective-permute-start.20 = (f32[392,384]{1,0:T(8,128)S(1)}, f32[392,384]{1,0:T(8,128)S(1)}, u32[]{:S(2)}, u32[]{:S(2)}) collective-permute-start(f32[392,384]{1,0:T(8,128)S(1)} %get-tuple-element.40), channel_id=1, source_target_pairs={{0,24},{8,0},{16,8},{24,16},{1,25},{9,1},{17,9},{25,17},{2,26},{10... | collective-permute-start | bytes 1806344 | tf_op jit(solution)/shard_map/ppermute | solution.py:39
  54.4 55.1 %collective-permute-start.21 = (f32[392,384]{1,0:T(8,128)S(1)}, f32[392,384]{1,0:T(8,128)S(1)}, u32[]{:S(2)}, u32[]{:S(2)}) collective-permute-start(f32[392,384]{1,0:T(8,128)S(1)} %get-tuple-element.40), channel_id=1, source_target_pairs={{0,8},{8,16},{16,24},{24,0},{1,9},{9,17},{17,25},{25,1},{2,10},{10... | collective-permute-start | bytes 1806344 | tf_op jit(solution)/shard_map/ppermute | solution.py:39
  54.4 55.1 %collective-permute-start.17 = (f32[392,384]{1,0:T(8,128)S(1)}, f32[392,384]{1,0:T(8,128)S(1)}, u32[]{:S(2)}, u32[]{:S(2)}) collective-permute-start(f32[392,384]{1,0:T(8,128)S(1)} %get-tuple-element.40), channel_id=1, source_target_pairs={{0,4},{4,0},{1,5},{5,1},{2,6},{6,2},{3,7},{7,3},{8,12},{12,8},{9,1... | collective-permute-start | bytes 1806344 | tf_op jit(solution)/shard_map/ppermute | solution.py:39
  67.3 25.8 %collective-permute-start.14 = (f32[384,384]{1,0:T(8,128)S(1)}, f32[384,384]{1,0:T(8,128)S(1)}, u32[]{:S(2)}, u32[]{:S(2)}) collective-permute-start(f32[384,384]{1,0:T(8,128)S(1)} %get-tuple-element.37.refs_12_), channel_id=1, source_target_pairs={{0,1},{1,0},{2,3},{3,2},{4,5},{5,4},{6,7},{7,6},{8,9},{9,8},{10,11... | collective-permute-start | bytes 1769480 | tf_op jit(solution)/shard_map/ppermute | solution.py:48
  79.3 28.6 %collective-permute-start.15 = (f32[384,384]{1,0:T(8,128)S(1)}, f32[384,384]{1,0:T(8,128)S(1)}, u32[]{:S(2)}, u32[]{:S(2)}) collective-permute-start(f32[384,384]{1,0:T(8,128)S(1)} %get-tuple-element.37.refs_12_), channel_id=1, source_target_pairs={{0,3},{1,2},{2,1},{3,0},{4,7},{5,6},{6,5},{7,4},{8,11},{9,10},{10,... | collective-permute-start | bytes 1769480 | tf_op jit(solution)/shard_map/ppermute | solution.py:48
  93.1 28.5 %collective-permute-start.18 = (f32[384,384]{1,0:T(8,128)S(1)}, f32[384,384]{1,0:T(8,128)S(1)}, u32[]{:S(2)}, u32[]{:S(2)}) collective-permute-start(f32[384,384]{1,0:T(8,128)S(1)} %get-tuple-element.36.square_ref), channel_id=1, source_target_pairs={{0,24},{8,0},{16,8},{24,16},{1,25},{9,1},{17,9},{25,17},{2,26},{10... | collective-permute-start | bytes 1769480 | tf_op jit(solution)/shard_map/ppermute | solution.py:39
  107.9 13.6 %collective-permute-start.19 = (f32[384,384]{1,0:T(8,128)S(1)}, f32[384,384]{1,0:T(8,128)S(1)}, u32[]{:S(2)}, u32[]{:S(2)}) collective-permute-start(f32[384,384]{1,0:T(8,128)S(1)} %get-tuple-element.36.square_ref), channel_id=1, source_target_pairs={{0,8},{8,16},{16,24},{24,0},{1,9},{9,17},{17,25},{25,1},{2,10},{10... | collective-permute-start | bytes 1769480 | tf_op jit(solution)/shard_map/ppermute | solution.py:39
  107.9 15.9 %collective-permute-start.16 = (f32[384,384]{1,0:T(8,128)S(1)}, f32[384,384]{1,0:T(8,128)S(1)}, u32[]{:S(2)}, u32[]{:S(2)}) collective-permute-start(f32[384,384]{1,0:T(8,128)S(1)} %get-tuple-element.36.square_ref), channel_id=1, source_target_pairs={{0,4},{4,0},{1,5},{5,1},{2,6},{6,2},{3,7},{7,3},{8,12},{12,8},{9,1... | collective-permute-start | bytes 1769480 | tf_op jit(solution)/shard_map/ppermute | solution.py:39
  109.4 16.5 %collective-permute-start.12 = (f32[384,384]{1,0:T(8,128)S(1)}, f32[384,384]{1,0:T(8,128)S(1)}, u32[]{:S(2)}, u32[]{:S(2)}) collective-permute-start(f32[384,384]{1,0:T(8,128)S(1)} %get-tuple-element.36.square_ref), channel_id=1, source_target_pairs={{0,1},{1,0},{2,3},{3,2},{4,5},{5,4},{6,7},{7,6},{8,9},{9,8},{10,11... | collective-permute-start | bytes 1769480 | tf_op jit(solution)/shard_map/ppermute | solution.py:48
  109.4 28.7 %collective-permute-start.13 = (f32[384,384]{1,0:T(8,128)S(1)}, f32[384,384]{1,0:T(8,128)S(1)}, u32[]{:S(2)}, u32[]{:S(2)}) collective-permute-start(f32[384,384]{1,0:T(8,128)S(1)} %get-tuple-element.36.square_ref), channel_id=1, source_target_pairs={{0,3},{1,2},{2,1},{3,0},{4,7},{5,6},{6,5},{7,4},{8,11},{9,10},{10,... | collective-permute-start | bytes 1769480 | tf_op jit(solution)/shard_map/ppermute | solution.py:48
